TPU v7x, 256 devices: a whole 4x4x8 slice. The times are simulated.
256 devices in a mesh: tok: 64 (over z, y, core), rep: 4 (over x).
Axes of the slice: x: 4, y: 4, z: 8, core: 2. Of those that a mesh axis runs over, the one named last changes fastest.
Arguments:
- patches: bfloat16 [65536, 768], P(('tok', 'rep')), may hold values from -6 to 6
- patch_view: int32 [65536], P(('tok', 'rep')), may hold values from 0 to 511
- rays: bfloat16 [65536, 768], P(('tok', 'rep')), may hold values from -24 to 24
- ray_view: int32 [65536], P(('tok', 'rep')), may hold values from 0 to 511
- targets: float32 [3, 65536], P(None, ('tok', 'rep')), may hold values from -6 to 6
- camera: bfloat16 [512, 768], P('tok'), may hold values from -6 to 6
- slots_init: float32 [64, 768], replicated, may hold values from -6 to 6
- key_weight: bfloat16 [768, 768], P('tok'), may hold values from -0.875 to 0.875
- value_weight: bfloat16 [768, 768], P('tok'), may hold values from -0.4375 to 0.4375
- query_weight: bfloat16 [768, 768], P('tok'), may hold values from -0.21875 to 0.21875
- gru_input: bfloat16 [768, 2304], P('tok'), may hold values from -0.21875 to 0.21875
- gru_hidden: bfloat16 [768, 2304], P('tok'), may hold values from -0.21875 to 0.21875
- mix_query: bfloat16 [768, 768], P('tok'), may hold values from -0.875 to 0.875
- mix_key: bfloat16 [768, 768], P('tok'), may hold values from -0.21875 to 0.21875
- render_in: bfloat16 [768, 1536], P('tok'), may hold values from -0.21875 to 0.21875
- render_out: bfloat16 [3, 1536], P(None, 'tok'), may hold values from -0.15625 to 0.15625
Outputs:
- slots_out: float32 [64, 768], replicated
- colour: float32 [3, 65536], P(None, ('tok', 'rep'))
- loss: float32 [], replicated
- grad_render_in: float32 [768, 1536], P('tok')
- grad_render_out: float32 [3, 1536], replicated
All inputs are finite; a program needn't handle non-finite values.
Results may differ from a plain program's by a relative error of at most 0.019.
Values may be sent and summed in bfloat16 or wider, within the bound.
A program may use at most 128 MiB of HBM per device.

v0:
```python
import jax
import jax.numpy as jnp
from jax import lax
from jax.sharding import Mesh
from jax.sharding import PartitionSpec as P

ITERS = 3
TOK = ("tok_0", "tok_1", "tok_2")
TOK_REP = ("tok_0", "tok_1", "tok_2", "rep")


EPSILON = 1e-05
ATTN_FLOOR = 1e-08


def from_everyone(value, axis):
    size = lax.axis_size(axis)
    return lax.all_to_all(
        jnp.broadcast_to(value[None], (size, *value.shape)), axis, 0, 0, tiled=True
    )


def in_order(parts, dim):
    parts = jnp.moveaxis(parts, 0, dim)
    lengths = parts.shape
    return parts.reshape(*lengths[:dim], lengths[dim] * lengths[dim + 1], *lengths[dim + 2 :])


def gathered_copies(value, axis, dim):
    parts = from_everyone(value, axis)
    return in_order(parts, dim)


def in_one_piece(arrays, axis, dim, along):
    both = jnp.concatenate(arrays, axis=along)
    filled, at, gathered = (lax.all_gather(both, axis, axis=dim, tiled=True), 0, [])
    for a in arrays:
        gathered.append(lax.slice_in_dim(filled, at, at + a.shape[along], axis=along))
        at += a.shape[along]
    return tuple(gathered)


def in_blocks(value, dim, size):
    lengths = value.shape
    parts = value.reshape(*lengths[:dim], size, lengths[dim] // size, *lengths[dim + 1 :])
    return jnp.moveaxis(parts, dim, 0)


def summed_on_arrival(value, axis, dim):
    size = lax.axis_size(axis)
    parts = lax.all_to_all(in_blocks(value, dim, size), axis, 0, 0, tiled=True)
    return jnp.sum(parts, axis=0)


def sum_in_two_steps(value, axes, dim):
    far, near = axes
    parts = in_blocks(value, dim, lax.axis_size(far))
    nearer = summed_on_arrival(parts, near, dim + 1)
    arrived = lax.all_to_all(nearer, far, split_axis=0, concat_axis=0, tiled=True)
    return arrived.sum(axis=0)


def padded_to(lines, size):
    spare = -lines.shape[0] % size
    if not spare:
        return lines
    return jnp.concatenate([lines, jnp.zeros((spare, *lines.shape[1:]), lines.dtype)])


def gather_axes(value, axes, dim):
    far, near = axes
    parts = from_everyone(from_everyone(value, far), near)
    return in_order(parts.swapaxes(0, 1).reshape(-1, *value.shape), dim)


def total_of(value, axes):
    own = sum_in_two_steps(
        padded_to(value, lax.axis_size(axes[0]) * lax.axis_size(axes[1])), axes, 0
    )
    whole = gather_axes(own, axes, 0)
    return whole[: len(value)].reshape(value.shape)


def packed_total(arrays, axis):
    vector, at, gathered = (jnp.concatenate([a.reshape(-1) for a in arrays]), 0, [])
    subtotal = total_of(vector, axis)
    for a in arrays:
        gathered.append(subtotal[at : at + a.size].reshape(a.shape))
        at += a.size
    return tuple(gathered)


def gather_in_order(value, axes, sequence):
    parts = value[None]
    for k in sequence:
        parts = lax.all_gather(parts, axes[k], axis=0, tiled=True)
    carried = [lax.axis_size(axes[k]) for k in reversed(sequence)]
    parts = parts.reshape(*carried, *value.shape)
    turned = sorted(range(len(sequence)), key=lambda place: sequence[len(sequence) - 1 - place])
    return parts.transpose(*turned, *range(len(sequence), parts.ndim)).reshape(-1, *value.shape)


def gather_axes_2(value, axes, sequence, dim):
    return in_order(gather_in_order(value, axes, sequence), dim)


def by_axis(value, axes):
    for axis in axes:
        value = lax.psum(value, axis)
    return value


def normalize(values):
    mean = jnp.mean(values, axis=-1, keepdims=True)
    centred = values - mean
    spread = jnp.mean(centred * centred, axis=-1, keepdims=True)
    return centred * lax.rsqrt(spread + EPSILON)


def lookup(table, index):
    onehot = (index[:, None] == jnp.arange(table.shape[0], dtype=jnp.int32)[None, :]).astype(
        jnp.bfloat16
    )
    return jnp.dot(onehot, table, preferred_element_type=jnp.float32)


def slot_update(slots, update, gru_input, gru_hidden):
    width = slots.shape[1]
    from_update = jnp.dot(
        update.astype(jnp.bfloat16), gru_input, preferred_element_type=jnp.float32
    )
    from_state = jnp.dot(slots.astype(jnp.bfloat16), gru_hidden, preferred_element_type=jnp.float32)
    reset = jax.nn.sigmoid(from_update[:, :width] + from_state[:, :width])
    blend = jax.nn.sigmoid(from_update[:, width : 2 * width] + from_state[:, width : 2 * width])
    candidate = jnp.tanh(from_update[:, 2 * width :] + reset * from_state[:, 2 * width :])
    return (1.0 - blend) * candidate + blend * slots


def add_rows(left, piece):
    return jnp.dot(left, piece, preferred_element_type=jnp.float32)


def on_device(
    patches,
    patch_view,
    rays,
    ray_view,
    targets,
    camera,
    slots_init,
    key_weight,
    value_weight,
    query_weight,
    gru_input,
    gru_hidden,
    mix_query,
    mix_key,
    render_in,
    render_out,
):
    width = patches.shape[1]
    scale = width ** (-0.5)
    table = gathered_copies(camera, TOK, 0)
    patch_in = patches.astype(jnp.float32) + lookup(table, patch_view)
    patch_x = normalize(patch_in).astype(jnp.bfloat16)
    pieces = in_one_piece((key_weight, value_weight), TOK, 0, 1)
    keys_sum = add_rows(patch_x, pieces[0])
    values_sum = add_rows(patch_x, pieces[1])
    keys = keys_sum.astype(jnp.bfloat16)
    values = values_sum.astype(jnp.bfloat16)
    query_full, input_full, hidden_full, mixkey_full, colour_full = (
        *in_one_piece((query_weight, gru_input, gru_hidden, mix_key), TOK, 0, 1),
        lax.all_gather(render_out, TOK, axis=1, tiled=True),
    )
    slots = slots_init
    for step in range(ITERS):
        query = (
            jnp.dot(
                normalize(slots).astype(jnp.bfloat16),
                query_full,
                preferred_element_type=jnp.float32,
            )
            * scale
        ).astype(jnp.bfloat16)
        logits = lax.dot_general(
            keys, query, (((1,), (1,)), ((), ())), preferred_element_type=jnp.float32
        )
        attn = jax.nn.softmax(logits, axis=1) + ATTN_FLOOR
        numer = lax.dot_general(
            attn.astype(jnp.bfloat16),
            values,
            (((0,), (0,)), ((), ())),
            preferred_element_type=jnp.float32,
        )
        denom = jnp.sum(attn, axis=0)
        numer, denom = packed_total((numer, denom), (("tok_0", "tok_1"), ("tok_2", "rep")))
        slots = slot_update(slots, numer / denom[:, None], input_full, hidden_full)
    slots_low = slots.astype(jnp.bfloat16)
    ray_in = rays.astype(jnp.float32) + lookup(table, ray_view)
    ray_x = ray_in.astype(jnp.bfloat16)
    ray_rows = ray_x.shape[0]
    query_sum = add_rows(ray_x, gather_axes_2(mix_query, TOK, (1, 0, 2), 0))
    ray_query = (query_sum * scale).astype(jnp.bfloat16)
    slot_keys = jnp.dot(slots_low, mixkey_full, preferred_element_type=jnp.float32).astype(
        jnp.bfloat16
    )
    mix_logits = lax.dot_general(
        ray_query, slot_keys, (((1,), (1,)), ((), ())), preferred_element_type=jnp.float32
    )
    mix = jax.nn.softmax(mix_logits, axis=1).astype(jnp.bfloat16)
    joined = (jnp.dot(mix, slots_low, preferred_element_type=jnp.float32) + ray_in).astype(
        jnp.bfloat16
    )
    pre = add_rows(joined, gather_axes(render_in, (("tok_0", "tok_1"), "tok_2"), 0))
    hidden = jax.nn.silu(pre).astype(jnp.bfloat16)
    colour = lax.dot_general(
        colour_full, hidden, (((1,), (1,)), ((), ())), preferred_element_type=jnp.float32
    )
    error = colour - targets
    rays_total = ray_rows * lax.axis_size(TOK) * lax.axis_size("rep")
    dcol = (error * (2.0 / jnp.sqrt(jnp.float32(3.0 * rays_total)))).astype(jnp.bfloat16)
    squared = jnp.sum(error * error)
    out_part = jnp.dot(dcol, hidden, preferred_element_type=jnp.float32)
    squared, grad_render_out = (by_axis(squared, TOK_REP), by_axis(out_part, TOK_REP))
    loss = squared / (3.0 * rays_total)
    dhidden = lax.dot_general(
        dcol, colour_full, (((0,), (0,)), ((), ())), preferred_element_type=jnp.float32
    )
    sig = jax.nn.sigmoid(pre)
    dpre = (dhidden * (sig + pre * sig * (1.0 - sig))).astype(jnp.bfloat16)
    mine = sum_in_two_steps(
        lax.dot_general(joined, dpre, (((0,), (0,)), ((), ())), preferred_element_type=jnp.float32),
        (("tok_0", "tok_1"), ("tok_2", "rep")),
        0,
    )
    grad_render_in = gathered_copies(mine, "rep", 0)
    return (slots, colour, loss, grad_render_in, grad_render_out)


def solution(mesh):
    torus = Mesh(
        mesh.devices.reshape(8, 4, 2, mesh.shape["rep"]), ("tok_0", "tok_1", "tok_2", "rep")
    )
    return jax.shard_map(
        on_device,
        mesh=torus,
        in_specs=(
            P(TOK_REP, None),
            P(TOK_REP),
            P(TOK_REP, None),
            P(TOK_REP),
            P(None, TOK_REP),
            P(TOK, None),
            P(),
            P(TOK, None),
            P(TOK, None),
            P(TOK, None),
            P(TOK, None),
            P(TOK, None),
            P(TOK, None),
            P(TOK, None),
            P(TOK, None),
            P(None, TOK),
        ),
        out_specs=(P(), P(None, TOK_REP), P(), P(TOK, None), P()),
        check_vma=False,
    )
```

profile of v0, /device:TPU:1, one launch (start us, length us, event | category | flops | bytes accessed | tf_op | source)
XLA Modules:
  0.0 690.0 jit_solution(10916712915491983667)
XLA Ops:
  13.0 13.1 %all-to-all-start = ((bf16[64,8,768]{2,1,0:T(8,128)(2,1)}), bf16[64,8,768]{2,1,0:T(8,128)(2,1)S(1)}, u32[]{:S(2)}, u32[]{:S(2)}) async-start(bf16[64,8,768]{2,1,0:T(8,128)(2,1)} %broadcast_in_dim.28), calls=%async_computation | async-start | bytes 1572864 | tf_op jit(solution)/shard_map/all_to_all | solution.py:18
  26.4 24.0 %all-to-all-done = bf16[64,8,768]{2,1,0:T(8,128)(2,1)S(1)} async-done(((bf16[64,8,768]{2,1,0:T(8,128)(2,1)}), bf16[64,8,768]{2,1,0:T(8,128)(2,1)S(1)}, u32[]{:S(2)}, u32[]{:S(2)}) %all-to-all-start) | async-done | bytes 786464 | tf_op jit(solution)/shard_map/all_to_all | solution.py:18
  51.2 43.6 %all-gather.11.cloned.1.call-done = bf16[64,12,1536]{2,1,0:T(8,128)(2,1)} async-done(((bf16[1,12,1536]{2,1,0:T(8,128)(2,1)}), bf16[64,12,1536]{2,1,0:T(8,128)(2,1)}) %all-gather.11.cloned.1.call-update) | async-done | bytes 2359312 | tf_op jit(solution)/shard_map/all_gather | solution.py:36
  94.8 4.9 reshape.143
  102.3 82.9 %all-gather.13.cloned.1.call-done = bf16[64,12,6144]{2,1,0:T(8,128)(2,1)} async-done(((bf16[1,12,6144]{2,1,0:T(8,128)(2,1)}), bf16[64,12,6144]{2,1,0:T(8,128)(2,1)}) %all-gather.13.cloned.1.call-update) | async-done | bytes 9437200 | tf_op jit(solution)/shard_map/all_gather | solution.py:36
  185.1 13.7 %reshape.145 = bf16[768,6144]{1,0:T(8,128)(2,1)} reshape(bf16[64,12,6144]{2,1,0:T(8,128)(2,1)} %all-gather.13.cloned.1.call-done) | data formatting | bytes 18874368
  201.7 10.8 %all_to_all.105 = f32[8,32,193]{2,1,0:T(8,128)S(1)} all-to-all(f32[8,32,193]{2,1,0:T(8,128)S(1)} %copy.54), channel_id=1, replica_groups=mesh['tok_0'=8,'tok_1'=4,'tok_2'=2,'rep'=4] {'tok_2','rep'}, dimensions={0} | all-to-all | bytes 395264 | tf_op jit(solution)/shard_map/all_to_all | solution.py:51
  212.5 13.7 %all_to_all.106 = f32[32,1,193]{2,1,0:T(1,128)S(1)} all-to-all(f32[32,1,193]{2,1,0:T(1,128)S(1)} %all_to_all.68), channel_id=1, replica_groups=mesh['tok_0'=8,'tok_1'=4,'tok_2'=2,'rep'=4] {'tok_0','tok_1'}, dimensions={0} | all-to-all | bytes 49408 | tf_op jit(solution)/shard_map/all_to_all | solution.py:59
  226.3 11.6 %all_to_all.107 = f32[32,1,193]{2,1,0:T(1,128)S(1)} all-to-all(f32[32,1,193]{2,1,0:T(1,128)S(1)} %broadcast_in_dim.29), channel_id=1, replica_groups=mesh['tok_0'=8,'tok_1'=4,'tok_2'=2,'rep'=4] {'tok_0','tok_1'}, dimensions={0} | all-to-all | bytes 49408 | tf_op jit(solution)/shard_map/all_to_all | solution.py:18
  238.6 6.2 all-to-all-start.4
  258.0 9.7 %all_to_all.108 = f32[8,32,193]{2,1,0:T(8,128)S(1)} all-to-all(f32[8,32,193]{2,1,0:T(8,128)S(1)} %copy.56), channel_id=1, replica_groups=mesh['tok_0'=8,'tok_1'=4,'tok_2'=2,'rep'=4] {'tok_2','rep'}, dimensions={0} | all-to-all | bytes 395264 | tf_op jit(solution)/shard_map/all_to_all | solution.py:51
  267.8 11.6 %all_to_all.109 = f32[32,1,193]{2,1,0:T(1,128)S(1)} all-to-all(f32[32,1,193]{2,1,0:T(1,128)S(1)} %all_to_all.73), channel_id=1, replica_groups=mesh['tok_0'=8,'tok_1'=4,'tok_2'=2,'rep'=4] {'tok_0','tok_1'}, dimensions={0} | all-to-all | bytes 49408 | tf_op jit(solution)/shard_map/all_to_all | solution.py:59
  279.5 11.6 %all_to_all.110 = f32[32,1,193]{2,1,0:T(1,128)S(1)} all-to-all(f32[32,1,193]{2,1,0:T(1,128)S(1)} %broadcast_in_dim.32), channel_id=1, replica_groups=mesh['tok_0'=8,'tok_1'=4,'tok_2'=2,'rep'=4] {'tok_0','tok_1'}, dimensions={0} | all-to-all | bytes 49408 | tf_op jit(solution)/shard_map/all_to_all | solution.py:18
  291.8 5.9 all-to-all-start.8
  311.1 9.9 %all_to_all.111 = f32[8,32,193]{2,1,0:T(8,128)} all-to-all(f32[8,32,193]{2,1,0:T(8,128)S(1)} %copy.58), channel_id=1, replica_groups=mesh['tok_0'=8,'tok_1'=4,'tok_2'=2,'rep'=4] {'tok_2','rep'}, dimensions={0} | all-to-all | bytes 395264 | tf_op jit(solution)/shard_map/all_to_all | solution.py:51
  322.3 4.0 all-to-all-start.13
  326.4 11.4 %all-gather.3 = bf16[4,12,768]{2,1,0:T(8,128)(2,1)S(1)} all-gather(bf16[1,12,768]{2,1,0:T(8,128)(2,1)S(1)} %bitcast.72), channel_id=2, replica_groups=mesh['tok_0'=8,'tok_1'=4,'tok_2'=2,'rep'=4] {'tok_1'}, dimensions={0}, use_global_device_ids=true | all-gather | bytes 92160 | tf_op jit(solution)/shard_map/all_gather | solution.py:96
  337.8 40.8 %all_gather.21 = bf16[32,12,768]{2,1,0:T(8,128)(2,1)S(1)} all-gather(bf16[4,12,768]{2,1,0:T(8,128)(2,1)S(1)} %all-gather.3), channel_id=1, replica_groups=mesh['tok_0'=8,'tok_1'=4,'tok_2'=2,'rep'=4] {'tok_0'}, dimensions={0}, use_global_device_ids=true | all-gather | bytes 663552 | tf_op jit(solution)/shard_map/all_gather | solution.py:96
  381.2 8.2 %all-to-all-start.10 = ((f32[32,1,193]{2,1,0:T(1,128)}), f32[32,1,193]{2,1,0:T(1,128)S(1)}, u32[]{:S(2)}, u32[]{:S(2)}) async-start(f32[32,1,193]{2,1,0:T(1,128)} %all_to_all.78), calls=%async_computation.10 | async-start | bytes 65536 | tf_op jit(solution)/shard_map/all_to_all | solution.py:59
  389.4 50.4 %all-gather.4 = bf16[64,24,3]{1,2,0:T(4,128)(2,1)S(1)} all-gather(bf16[1,24,3]{1,2,0:T(4,128)(2,1)S(1)} %bitcast.73), channel_id=1, replica_groups=mesh['tok_0'=8,'tok_1'=4,'tok_2'=2,'rep'=4] {'tok_0','tok_1','tok_2'}, dimensions={0}, use_global_device_ids=true | all-gather | bytes 9360 | tf_op jit(solution)/shard_map/all_gather | solution.py:173
  454.1 4.1 all-to-all-start.14
  461.5 6.7 all-to-all-start.11
  477.7 5.1 all-to-all-start.12
  500.9 5.0 fusion.12
  505.9 7.9 %reshape_reshape.35 = f32[32,8,3,1536]{3,2,1,0:T(4,128)} reshape(f32[768,1536]{1,0:T(8,128)} %fusion.12) | data formatting | bytes 9437184 | tf_op jit(solution)/shard_map/reshape;reshape | solution.py:45
  513.8 5.5 copy.65
  519.3 57.9 %all_to_all.112 = f32[8,32,3,1536]{3,1,2,0:T(8,128)} all-to-all(f32[8,32,3,1536]{3,1,2,0:T(8,128)S(1)} %copy.65), channel_id=1, replica_groups=mesh['tok_0'=8,'tok_1'=4,'tok_2'=2,'rep'=4] {'tok_2','rep'}, dimensions={0} | all-to-all | bytes 9437184 | tf_op jit(solution)/shard_map/all_to_all | solution.py:51
  580.4 28.3 %all_to_all.113 = f32[32,3,1536]{2,1,0:T(4,128)S(1)} all-to-all(f32[32,3,1536]{2,1,0:T(4,128)S(1)} %copy.66), channel_id=1, replica_groups=mesh['tok_0'=8,'tok_1'=4,'tok_2'=2,'rep'=4] {'tok_0','tok_1'}, dimensions={0} | all-to-all | bytes 1179648 | tf_op jit(solution)/shard_map/all_to_all | solution.py:59
  613.0 21.7 %all-reduce = (f32[]{:T(128)}, f32[3,1536]{1,0:T(4,128)S(1)}) all-reduce(f32[]{:T(128)} %get-tuple-element.18, f32[3,1536]{1,0:T(4,128)S(1)} %fusion.145), channel_id=1, replica_groups=mesh['tok_0'=8,'tok_1'=4,'tok_2'=2,'rep'=4] {'tok_0'}, use_global_device_ids=true, to_apply=%region_26.27 | all-reduce | flops 4609 | bytes 36872 | tf_op jit(solution)/shard_map/psum | solution.py:109
  634.6 14.1 %all-reduce.2 = (f32[]{:T(128)}, f32[3,1536]{1,0:T(4,128)S(1)}) all-reduce(f32[]{:T(128)} %get-tuple-element.5, f32[3,1536]{1,0:T(4,128)S(1)} %get-tuple-element.6), channel_id=1, replica_groups=mesh['tok_0'=8,'tok_1'=4,'tok_2'=2,'rep'=4] {'tok_1'}, use_global_device_ids=true, to_apply=%region_27.28 | all-reduce | flops 4609 | bytes 36872 | tf_op jit(solution)/shard_map/psum | solution.py:109
  648.8 16.4 %all-reduce.3 = (f32[]{:T(128)}, f32[3,1536]{1,0:T(4,128)S(1)}) all-reduce(f32[]{:T(128)} %get-tuple-element.9, f32[3,1536]{1,0:T(4,128)S(1)} %get-tuple-element.10), channel_id=1, replica_groups=mesh['tok_0'=8,'tok_1'=4,'tok_2'=2,'rep'=4] {'tok_2'}, use_global_device_ids=true, to_apply=%region_28.29 | all-reduce | flops 4609 | bytes 36872 | tf_op jit(solution)/shard_map/psum | solution.py:109
  665.2 14.9 %all-reduce.1 = (f32[]{:T(128)}, f32[3,1536]{1,0:T(4,128)}) all-reduce(f32[]{:T(128)} %get-tuple-element.11, f32[3,1536]{1,0:T(4,128)S(1)} %get-tuple-element.12), channel_id=1, replica_groups=mesh['tok_0'=8,'tok_1'=4,'tok_2'=2,'rep'=4] {'rep'}, use_global_device_ids=true, to_apply=%region_29.30 | all-reduce | flops 4609 | bytes 36872 | tf_op jit(solution)/shard_map/psum | solution.py:109
  (154 shorter events, 96.4 us)
Async XLA Ops:
  8.0 18.1 %copy-start.3 = (f32[64,768]{1,0:T(8,128)S(1)}, f32[64,768]{1,0:T(8,128)}, u32[]{:S(2)}) copy-start(f32[64,768]{1,0:T(8,128)} %param.22) | copy-start | bytes 589828
  8.0 42.5 %copy-start.11 = (s32[256]{0:T(256)S(1)}, s32[256]{0:T(256)}, u32[]{:S(2)}) copy-start(s32[256]{0:T(256)} %param.17) | copy-start | bytes 3076
  8.0 42.5 %copy-start.6 = (bf16[256,768]{1,0:T(8,128)(2,1)S(1)}, bf16[256,768]{1,0:T(8,128)(2,1)}, u32[]{:S(2)}) copy-start(bf16[256,768]{1,0:T(8,128)(2,1)} %param.16) | copy-start | bytes 1179652
  8.0 86.8 %all-gather.11.cloned.1.call-start = ((), (), s32[]{:S(2)}) async-start(), calls=%async_computation.19 | async-start | bytes 3194880 | tf_op jit(solution)/shard_map/all_gather | solution.py:36
  9.6 175.6 %all-gather.13.cloned.1.call-start = ((), (), s32[]{:S(2)}) async-start(), calls=%async_computation.20 | async-start | bytes 12779520 | tf_op jit(solution)/shard_map/all_gather | solution.py:36
  13.0 37.5 %all-to-all-start = ((bf16[64,8,768]{2,1,0:T(8,128)(2,1)}), bf16[64,8,768]{2,1,0:T(8,128)(2,1)S(1)}, u32[]{:S(2)}, u32[]{:S(2)}) async-start(bf16[64,8,768]{2,1,0:T(8,128)(2,1)} %broadcast_in_dim.28), calls=%async_computation | async-start | bytes 1572864 | tf_op jit(solution)/shard_map/all_to_all | solution.py:18
  99.7 2.0 copy-start.4
  102.3 153.0 %copy-start.13 = (bf16[256,768]{1,0:T(8,128)(2,1)}, bf16[256,768]{1,0:T(8,128)(2,1)S(1)}, u32[]{:S(2)}) copy-start(bf16[256,768]{1,0:T(8,128)(2,1)S(1)} %convolution_convert_fusion.1) | copy-start | bytes 1179652
  238.6 12.7 %all-to-all-start.4 = ((f32[8,32,193]{2,1,0:T(8,128)}), f32[8,32,193]{2,1,0:T(8,128)S(1)}, u32[]{:S(2)}, u32[]{:S(2)}) async-start(f32[8,32,193]{2,1,0:T(8,128)} %broadcast_in_dim.31), calls=%async_computation.4 | async-start | bytes 524288 | tf_op jit(solution)/shard_map/all_to_all | solution.py:18
  291.8 12.5 %all-to-all-start.8 = ((f32[8,32,193]{2,1,0:T(8,128)}), f32[8,32,193]{2,1,0:T(8,128)S(1)}, u32[]{:S(2)}, u32[]{:S(2)}) async-start(f32[8,32,193]{2,1,0:T(8,128)} %broadcast_in_dim.34), calls=%async_computation.8 | async-start | bytes 524288 | tf_op jit(solution)/shard_map/all_to_all | solution.py:18
  308.1 12.8 %copy-start.7 = (bf16[12,1536]{1,0:T(8,128)(2,1)S(1)}, bf16[12,1536]{1,0:T(8,128)(2,1)}, u32[]{:S(2)}) copy-start(bf16[12,1536]{1,0:T(8,128)(2,1)} %param.30) | copy-start | bytes 110596
  321.0 5.4 copy-start.8
  322.3 58.9 %all-to-all-start.13 = ((bf16[32,12,1536]{2,1,0:T(8,128)(2,1)}), bf16[32,12,1536]{2,1,0:T(8,128)(2,1)S(1)}, u32[]{:S(2)}, u32[]{:S(2)}) async-start(bf16[32,12,1536]{2,1,0:T(8,128)(2,1)} %broadcast_in_dim.39), calls=%async_computation.13 | async-start | bytes 3145728 | tf_op jit(solution)/shard_map/all_to_all | solution.py:18
  326.3 63.1 %copy-start.12 = (bf16[3,24]{1,0:T(4,128)(2,1)S(1)}, bf16[3,24]{1,0:T(4,128)(2,1)}, u32[]{:S(2)}) copy-start(bf16[3,24]{1,0:T(4,128)(2,1)} %param.31) | copy-start | bytes 436
  326.3 113.7 %all-gather.9.cloned.1.call-start = ((), (), s32[]{:S(2)}) async-start(), calls=%async_computation.18 | async-start | bytes 1769472 | tf_op jit(solution)/shard_map/all_gather | solution.py:96
  381.2 69.9 %all-to-all-start.10 = ((f32[32,1,193]{2,1,0:T(1,128)}), f32[32,1,193]{2,1,0:T(1,128)S(1)}, u32[]{:S(2)}, u32[]{:S(2)}) async-start(f32[32,1,193]{2,1,0:T(1,128)} %all_to_all.78), calls=%async_computation.10 | async-start | bytes 65536 | tf_op jit(solution)/shard_map/all_to_all | solution.py:59
  454.1 14.2 %copy-start.10 = (s32[256]{0:T(256)S(1)}, s32[256]{0:T(256)}, u32[]{:S(2)}) copy-start(s32[256]{0:T(256)} %param.19) | copy-start | bytes 3076
  454.1 6.8 all-to-all-start.14
  460.9 9.7 %copy-start = (bf16[2,32,12,1536]{3,1,2,0:T(8,128)(2,1)}, bf16[2,32,12,1536]{3,1,2,0:T(8,128)(2,1)S(1)}, u32[]{:S(2)}) copy-start(bf16[2,32,12,1536]{3,1,2,0:T(8,128)(2,1)S(1)} %all-to-all-done.14) | copy-start | bytes 7077892
  461.5 15.4 %all-to-all-start.11 = ((f32[32,1,193]{2,1,0:T(1,128)}), f32[32,1,193]{2,1,0:T(1,128)S(1)}, u32[]{:S(2)}, u32[]{:S(2)}) async-start(f32[32,1,193]{2,1,0:T(1,128)} %broadcast_in_dim.35), calls=%async_computation.11 | async-start | bytes 65536 | tf_op jit(solution)/shard_map/all_to_all | solution.py:18
  477.7 11.6 %all-to-all-start.12 = ((f32[8,32,193]{2,1,0:T(8,128)}), f32[8,32,193]{2,1,0:T(8,128)S(1)}, u32[]{:S(2)}, u32[]{:S(2)}) async-start(f32[8,32,193]{2,1,0:T(8,128)} %broadcast_in_dim.37), calls=%async_computation.12 | async-start | bytes 524288 | tf_op jit(solution)/shard_map/all_to_all | solution.py:18
  492.7 2.0 copy-start.1
  492.7 2.0 copy-start.2
  492.9 2.8 copy-start.5
  495.7 3.6 copy-start.9
  609.4 71.3 %all-to-all-start.17 = ((f32[4,3,1536]{2,1,0:T(4,128)}), f32[4,3,1536]{2,1,0:T(4,128)S(1)}, u32[]{:S(2)}, u32[]{:S(2)}) async-start(f32[4,3,1536]{2,1,0:T(4,128)} %broadcast_in_dim.41), calls=%async_computation.17 | async-start | bytes 196608 | tf_op jit(solution)/shard_map/all_to_all | solution.py:18
Sparse Core Ops, SparseCore 0:
  12.2 82.5 all-gather.10
  98.1 86.9 all-gather.12
Sparse Core Ops, SparseCore 1:
  379.7 18.3 all-gather.8
where the time goes:
time: 694 us; the launch traced here: 690 us
  blocking collectives  335 us (48%)
  waiting for transfers between devices  166 us (24%)
  local copies, waits for them, and re-layouts  64.1 us (9%)
  starting transfers between devices  56.8 us (8%)
  matrix products  41.2 us (6%)
  between operations  17.9 us (3%)
  other arithmetic  9.31 us (1%)
    all_gather x2, waiting for transfers between devices, in_one_piece(): lax.all_gather(both, axis, axis=dim, tiled=True)  126 us
    all_to_all x4, blocking collectives, summed_on_arrival(): parts = lax.all_to_all(in_blocks(value, dim, size), axis, 0, 0, tiled=True)  88.4 us
    psum x4, blocking collectives, by_axis(): value = lax.psum(value, axis)  67.1 us
    all_to_all x3, blocking collectives, sum_in_two_steps(): lax.all_to_all(nearer, far, split_axis=0, concat_axis=0, tiled=True)  53.6 us
    all_gather x2, blocking collectives, gather_in_order(): parts = lax.all_gather(parts, axes[k], axis=0, tiled=True)  52.2 us
    all_gather x1, blocking collectives, on_device(): lax.all_gather(render_out, TOK, axis=1, tiled=True)  50.4 us
    all_to_all x8, starting transfers between devices, from_everyone(): lax.all_to_all(jnp.broadcast_to(value[None], (size, *value.shape)), axis,...  48.4 us
    all_to_all x8, waiting for transfers between devices, from_everyone(): lax.all_to_all(jnp.broadcast_to(value[None], (size, *value.shape)), axis,...  39.3 us
  transfers between devices with their start and end apart: 12, of which 8 were waited for; matrix products, arithmetic and copies ran while one was open for 6% of the time, Pallas kernels for 0%

commit v1 on v0

v1 whole, which is shorter than its diff:
```python
import functools

import jax
import jax.numpy as jnp
from jax import lax
from jax.experimental import pallas as pl
from jax.experimental.pallas import tpu as pltpu
from jax.sharding import Mesh
from jax.sharding import PartitionSpec as P

ITERS = 3
EPSILON = 1e-05
ATTN_FLOOR = 1e-08
NZ, NY, NC, NX = 8, 4, 2, 4
BF = jnp.bfloat16
F32 = jnp.float32

OFF = (0, 1536, 3072, 7680)
LEN = (1536, 1536, 4608, 2560)
NB = 4


def dot(a, b, ca=1, cb=0):
    return lax.dot_general(a, b, (((ca,), (cb,)), ((), ())), preferred_element_type=F32)


def normalize(values):
    mean = jnp.mean(values, axis=-1, keepdims=True)
    centred = values - mean
    spread = jnp.mean(centred * centred, axis=-1, keepdims=True)
    return centred * lax.rsqrt(spread + EPSILON)


def onehot(mask):
    return mask.astype(F32).astype(BF)


def softmax0(logits):
    top = jnp.max(logits, axis=0, keepdims=True)
    e = jnp.exp(logits - top)
    return e / jnp.sum(e, axis=0, keepdims=True)


def rows(start, size):
    return pl.ds(pl.multiple_of(start, 16), size)


def lanes(start, size):
    return pl.ds(pl.multiple_of(start, 128), size)


def kernel(
    pview, rview, patches, rays, targets, slots_init, packed, camera,
    slots_out, colour_out, loss_out, gin_out, gro_out,
    cy0, cy1, cy2, cy3, f0, f1, f2, f3, sg0, sg1, sg2, sg3, camsg, camcy, camf,
    px, rin, rx, ro, state, tsend, trecv, tysend, tyrecv, tzsend, tzrecv,
    psend, precv, ssend, srecv, dcol8, small, smrecv_cx, smrecv_y, smrecv_z, smy, smz,
    jt, gown, gcs, gcr, gxs, gxr, gzs, gzr, gys, gyr, gfs, gfr,
    cy_s, cy_r, z_s, z_r, x_s, x_r, c_s, c_r, it_s, it_r, gr_s, gr_r,
):
    z, y, c, x = (lax.axis_index(a) for a in ("z", "y", "c", "x"))
    cyb, full, stage = (cy0, cy1, cy2, cy3), (f0, f1, f2, f3), (sg0, sg1, sg2, sg3)
    width = patches.shape[1]
    scale = width ** (-0.5)
    pending = []

    def send(src, dst, ssem, rsem, **where):
        cp = pltpu.make_async_remote_copy(
            src_ref=src, dst_ref=dst, send_sem=ssem, recv_sem=rsem,
            device_id=where, device_id_type=pl.DeviceIdType.MESH,
        )
        cp.start()
        pending.append(cp)
        return cp

    def yc_peers():
        return [(dy, dc) for dy in range(NY) for dc in range(NC) if dy or dc]

    def cx_peers():
        return [(dc, dx) for dc in range(NC) for dx in range(NX) if dc or dx]

    def flip(dc):
        return 1 - c if dc else c

    barrier = pltpu.get_barrier_semaphore()
    met = 0
    for dy, dc in yc_peers():
        pl.semaphore_signal(barrier, inc=1, device_id={"y": lax.rem(y + dy, NY), "c": flip(dc)}, device_id_type=pl.DeviceIdType.MESH)
        met += 1
    for dc, dx in cx_peers():
        if dx:
            pl.semaphore_signal(barrier, inc=1, device_id={"x": lax.rem(x + dx, NX), "c": flip(dc)}, device_id_type=pl.DeviceIdType.MESH)
            met += 1
    for dz in range(1, NZ):
        pl.semaphore_signal(barrier, inc=1, device_id={"z": lax.rem(z + dz, NZ)}, device_id_type=pl.DeviceIdType.MESH)
        met += 1
    pl.semaphore_wait(barrier, met)

    me_yc = y * 2 + c

    def start_yc(src, buf, slot):
        buf[rows(me_yc * 16, 16), :] = src[...]
        out = []
        for k, (dy, dc) in enumerate(yc_peers()):
            out.append(send(src, buf.at[rows(me_yc * 16, 16)], cy_s.at[slot, k], cy_r.at[slot, k],
                            y=lax.rem(y + dy, NY), c=flip(dc)))
        return out

    def start_bundle(b):
        w = LEN[b] // NX
        stage[b][...] = packed[:, lanes(OFF[b] + x * w, w)]
        return start_yc(stage[b], cyb[b], b)

    def compact(shards, real, first, count):
        r = lax.broadcasted_iota(jnp.int32, (count, 128), 0) + first
        k = lax.broadcasted_iota(jnp.int32, (count, 128), 1)
        lane = k % 16
        mask = (lane < real) & (r == (k // 16) * real + lane)
        return dot(onehot(mask), shards).astype(BF)

    def piece(b, zz):
        w = LEN[b] // NX
        return full[b].at[rows(zz * 96 + c * 48, 48), lanes(x * w, w)]

    def start_z(b, arrived):
        for cp in arrived:
            cp.wait()
        w = LEN[b] // NX
        full[b][rows(z * 96 + c * 48, 48), lanes(x * w, w)] = compact(cyb[b][...], 12, c * 48, 48)
        return [
            send(piece(b, z), piece(b, z), z_s.at[b, d], z_r.at[b, d], z=lax.rem(z + d, NZ))
            for d in range(1, NZ)
        ]

    def forward_x(b, ref, d):
        return [
            send(ref, ref, x_s.at[b, dx, d], x_r.at[b, dx, d], x=lax.rem(x + dx, NX))
            for dx in range(1, NX)
        ]

    def start_x(b, arriving):
        out = forward_x(b, piece(b, z), 0)
        for d in range(1, NZ):
            arriving[d - 1].wait()
            out += forward_x(b, piece(b, lax.rem(z - d + NZ, NZ)), d)
        return out

    def swap_core(b, arriving):
        for cp in arriving:
            cp.wait()
        cps = []
        for zz in range(NZ):
            ref = full[b].at[rows(zz * 96 + c * 48, 48)]
            cps.append(send(ref, ref, c_s.at[b, zz], c_r.at[b, zz], c=1 - c))
        return cps

    def done(cps):
        for cp in cps:
            cp.wait()

    cy_b0 = start_bundle(0)
    camsg[...] = camera[...]
    cy_cam = start_yc(camsg, camcy, 4)
    n0 = normalize(slots_init[...]).astype(BF)
    z_b0 = start_z(0, cy_b0)
    done(cy_cam)
    half = width // 2
    camf[rows(z * 64 + x * 16, 16), lanes(c * half, half)] = compact(camcy[:, lanes(c * half, half)], 8, x * 16, 16)

    def cam_piece(zz):
        return camf.at[rows(zz * 64 + x * 16, 16), lanes(c * half, half)]

    z_cam = [
        send(cam_piece(z), cam_piece(z), z_s.at[4, d], z_r.at[4, d], z=lax.rem(z + d, NZ))
        for d in range(1, NZ)
    ]
    cy_b2 = start_bundle(2)
    cy_b1 = start_bundle(1)
    x_cam = forward_x(4, cam_piece(z), 0)
    for d in range(1, NZ):
        z_cam[d - 1].wait()
        x_cam += forward_x(4, cam_piece(lax.rem(z - d + NZ, NZ)), d)
    x_b0 = start_x(0, z_b0)
    z_b2 = start_z(2, cy_b2)
    z_b1 = start_z(1, cy_b1)
    done(x_cam)
    cam_half = camf.at[:, lanes(c * half, half)]
    done([send(cam_half, cam_half, c_s.at[4, 0], c_r.at[4, 0], c=1 - c)])

    def lookup(view):
        v = lax.broadcasted_iota(jnp.int32, (camf.shape[0], view.shape[1]), 0)
        return dot(onehot(v == view[...]), camf[...], 0, 0)

    px[...] = normalize(patches[...].astype(F32) + lookup(pview)).astype(BF)
    rin[...] = rays[...].astype(F32) + lookup(rview)
    rx[...] = rin[...].astype(BF)
    done(swap_core(0, x_b0))

    def slot_projection(normed):
        query = (dot(normed, f0[:, 0:width]) * scale).astype(BF)
        return dot(query, f0[:, width : 2 * width], 1, 1).astype(BF)

    group = c * NX + x
    mine = pl.ds(pl.multiple_of(group * 8, 8), 8)
    state[...] = slots_init[mine, :]
    proj = slot_projection(n0)
    x_b1 = x_b2 = x_b3 = cy_b3 = z_b3 = c_b3 = None

    def group_rows(buf, t):
        return jnp.concatenate([buf[t, g].astype(F32) for g in range(8)], axis=0)

    def share(t, value):
        psend[t] = value
        precv[t, group] = value
        return [
            send(psend.at[t], precv.at[t, group], it_s.at[t, 24 + k], it_r.at[t, 24 + k],
                 c=flip(dc), x=lax.rem(x + dx, NX))
            for k, (dc, dx) in enumerate(cx_peers())
        ]

    for t in range(ITERS):
        attn = softmax0(dot(proj, px[...], 1, 1)) + ATTN_FLOOR
        total = dot(attn.astype(BF), px[...])
        denom = jnp.sum(attn, axis=1, keepdims=True)
        for g in range(8):
            tsend[t, g, :, 0:width] = total[8 * g : 8 * g + 8].astype(BF)
            tsend[t, g, :, width : width + 128] = jnp.broadcast_to(denom[8 * g : 8 * g + 8], (8, 128)).astype(BF)
        cps = []
        for k, (dc, dx) in enumerate(cx_peers()):
            cc, xx = flip(dc), lax.rem(x + dx, NX)
            cps.append(send(tsend.at[t, cc * NX + xx], trecv.at[t, k], it_s.at[t, k], it_r.at[t, k], c=cc, x=xx))
        if t == 0:
            x_b1 = start_x(1, z_b1)
            x_b2 = start_x(2, z_b2)
            cy_b3 = start_bundle(3)
        if t == 1:
            x_b3 = start_x(3, z_b3)
        if t == 2:
            c_b3 = swap_core(3, x_b3)
        acc = tsend[t, group].astype(F32)
        for k, cp in enumerate(cps):
            cp.wait()
            acc += trecv[t, k].astype(F32)
        tysend[t] = acc.astype(BF)
        cps = [
            send(tysend.at[t], tyrecv.at[t, d], it_s.at[t, 8 + d], it_r.at[t, 8 + d], y=lax.rem(y + d, NY))
            for d in range(1, NY)
        ]
        for cp in cps:
            cp.wait()
        acc = ordered(tyrecv, tysend, t, y, NY)
        tzsend[t] = acc.astype(BF)
        cps = [
            send(tzsend.at[t], tzrecv.at[t, d], it_s.at[t, 12 + d], it_r.at[t, 12 + d], z=lax.rem(z + d, NZ))
            for d in range(1, NZ)
        ]
        if t == 0:
            c_b1 = swap_core(1, x_b1)
            c_b2 = swap_core(2, x_b2)
            z_b3 = start_z(3, cy_b3)
        for cp in cps:
            cp.wait()
        acc = ordered(tzrecv, tzsend, t, z, NZ)
        if t == 0:
            done(c_b1)
            done(c_b2)
        mean_x = (acc[:, 0:width] / acc[:, width : width + 1]).astype(BF)
        update = dot(mean_x, f1[:, 0:width]).astype(BF)
        slots = state[...]
        a = dot(update, f2[:, 0 : 3 * width])
        b = dot(slots.astype(BF), f2[:, 3 * width : 6 * width])
        reset = jax.nn.sigmoid(a[:, 0:width] + b[:, 0:width])
        blend = jax.nn.sigmoid(a[:, width : 2 * width] + b[:, width : 2 * width])
        cand = jnp.tanh(a[:, 2 * width :] + reset * b[:, 2 * width :])
        slots = (1.0 - blend) * cand + blend * slots
        state[...] = slots
        if t + 1 < ITERS:
            cps = share(t, slot_projection(normalize(slots).astype(BF)))
            done(cps)
            proj = group_rows(precv, t).astype(BF)

    t = ITERS - 1
    ssend[...] = slots
    srecv[mine, :] = slots
    s_cps = [
        send(ssend, srecv.at[mine], gr_s.at[0, k], gr_r.at[0, k], c=flip(dc), x=lax.rem(x + dx, NX))
        for k, (dc, dx) in enumerate(cx_peers())
    ]
    done(c_b3)
    slot_keys = dot(slots.astype(BF), f1[:, width : 2 * width]).astype(BF)
    r_cps = share(t, (dot(slot_keys, f3[:, 0:width], 1, 1) * scale).astype(BF))
    r = lax.broadcasted_iota(jnp.int32, (width, 1), 0)
    hid = 2 * r - r % 12
    unit = lax.broadcasted_iota(jnp.int32, (width, 2 * width), 1)
    ro[...] = (
        dot(f3[:, 3 * width : 3 * width + 128], onehot(unit == hid), 0, 0)
        + dot(f3[:, 3 * width + 128 : 3 * width + 256], onehot(unit == hid + 12), 0, 0)
    )[0:8].astype(BF)
    done(s_cps)
    done(r_cps)
    slots_all = srecv[...]
    slots_out[...] = slots_all
    low = slots_all.astype(BF)
    mix = softmax0(dot(group_rows(precv, t).astype(BF), rx[...], 1, 1)).astype(BF)
    joined = (dot(mix, low, 0, 0) + rin[...]).astype(BF)
    pre = dot(joined, f3[:, width : 3 * width])
    sig = jax.nn.sigmoid(pre)
    hidden = (pre * sig).astype(BF)
    colour = dot(ro[...], hidden, 1, 1)[0:3]
    colour_out[...] = colour
    error = colour - targets[...]
    rays_total = rin.shape[0] * NZ * NY * NC * NX
    dcol8[...] = jnp.zeros_like(dcol8)
    dcol8[0:3, :] = error * (2.0 / jnp.sqrt(jnp.float32(3.0 * rays_total)))
    dcol = dcol8[...].astype(BF)
    dpre = (dot(dcol, ro[...], 0, 0) * (sig + pre * sig * (1.0 - sig))).astype(BF)
    gro = dot(dcol, hidden)
    squared = jnp.sum(jnp.sum(error * error, axis=1, keepdims=True), axis=0, keepdims=True)

    turned = jnp.transpose(joined.astype(F32)).astype(BF)
    for zz in range(NZ):
        for h in range(NC):
            jt[384 * h + 48 * zz : 384 * h + 48 * zz + 48, :] = turned[96 * zz + 48 * h : 96 * zz + 48 * h + 48]
    gcs[...] = dot(jt[rows(384 * (1 - c), 384), :], dpre).astype(BF)
    g_c = send(gcs, gcr, gr_s.at[1, 0], gr_r.at[1, 0], c=1 - c)
    small[...] = jnp.zeros_like(small)
    small[0:3, :] = gro[0:3, 0:width]
    small[3:6, :] = gro[0:3, width:]
    small[6:7, :] = jnp.broadcast_to(squared, (1, width))
    sm_cps = [
        send(small, smrecv_cx.at[group], gr_s.at[2, k], gr_r.at[2, k], c=flip(dc), x=lax.rem(x + dx, NX))
        for k, (dc, dx) in enumerate(cx_peers())
    ]
    smrecv_cx[group] = small[...]
    gown[...] = dot(jt[rows(384 * c, 384), :], dpre)
    g_c.wait()
    gown[...] += gcr[...].astype(F32)
    gxs[...] = gown[...].astype(BF)
    quarter = 2 * width // NX
    gx = [
        send(gxs.at[:, lanes(lax.rem(x + d, NX) * quarter, quarter)], gxr.at[d], gr_s.at[3, d], gr_r.at[3, d], x=lax.rem(x + d, NX))
        for d in range(1, NX)
    ]
    done(sm_cps)
    acc_s = sum_of(smrecv_cx, 8)
    smy[...] = acc_s
    smrecv_y[y] = acc_s
    sm_cps = [
        send(smy, smrecv_y.at[y], gr_s.at[4, d], gr_r.at[4, d], y=lax.rem(y + d, NY)) for d in range(1, NY)
    ]
    done(sm_cps)
    acc_s = sum_of(smrecv_y, NY)
    smz[...] = acc_s
    smrecv_z[z] = acc_s
    sm_cps = [
        send(smz, smrecv_z.at[z], gr_s.at[5, d], gr_r.at[5, d], z=lax.rem(z + d, NZ)) for d in range(1, NZ)
    ]
    acc_g = gown[:, lanes(x * quarter, quarter)]
    for d, cp in enumerate(gx):
        cp.wait()
        acc_g += gxr[d + 1].astype(F32)
    gzs[...] = acc_g.astype(BF)
    gz = [
        send(gzs.at[rows(lax.rem(z + d, NZ) * 48, 48)], gzr.at[d], gr_s.at[6, d], gr_r.at[6, d], z=lax.rem(z + d, NZ))
        for d in range(1, NZ)
    ]
    done(sm_cps)
    acc_s = sum_of(smrecv_z, NZ)
    gro_out[:, 0:width] = acc_s[0:3]
    gro_out[:, width:] = acc_s[3:6]
    loss_out[...] = acc_s[6:7, 0:1] / (3.0 * rays_total)
    acc_g = gzs[rows(z * 48, 48), :].astype(F32)
    for d, cp in enumerate(gz):
        cp.wait()
        acc_g += gzr[d + 1].astype(F32)
    gys[...] = acc_g
    for d in range(1, NY):
        to = lax.rem(y + d, NY)

        @pl.when(to // 2 == c)
        def _():
            pltpu.make_async_remote_copy(
                src_ref=gys, dst_ref=gyr.at[d], send_sem=gr_s.at[7, d], recv_sem=gr_r.at[7, d],
                device_id={"y": to}, device_id_type=pl.DeviceIdType.MESH,
            ).start()

    def final(k, dc, dx):
        return pltpu.make_async_remote_copy(
            src_ref=gfs, dst_ref=gfr.at[x], send_sem=gr_s.at[8, k], recv_sem=gr_r.at[8, dx],
            device_id={"c": flip(dc), "x": lax.rem(x + dx, NX)}, device_id_type=pl.DeviceIdType.MESH,
        )

    @pl.when(y // 2 == c)
    def _():
        acc = gys[...]
        for d in range(1, NY):
            pltpu.make_async_remote_copy(
                src_ref=gys, dst_ref=gyr.at[d], send_sem=gr_s.at[7, d], recv_sem=gr_r.at[7, d],
                device_id={"y": lax.rem(y + d, NY)}, device_id_type=pl.DeviceIdType.MESH,
            ).wait_recv()
            acc += gyr[d]
        part = jnp.where(y % 2 == 0, acc[0:24], acc[24:48])
        gfs[...] = part
        gfr[x] = part
        for k, (dc, dx) in enumerate(cx_peers()):
            final(k, dc, dx).start()

    for d in range(1, NY):
        to = lax.rem(y + d, NY)

        @pl.when(to // 2 == c)
        def _():
            pltpu.make_async_remote_copy(
                src_ref=gys, dst_ref=gyr.at[d], send_sem=gr_s.at[7, d], recv_sem=gr_r.at[7, d],
                device_id={"y": to}, device_id_type=pl.DeviceIdType.MESH,
            ).wait_send()

    @pl.when(y // 2 != c)
    def _():
        final(0, 0, 0).wait_recv()

    for dx in range(1, NX):
        final(0, 0, dx).wait_recv()
    for xx in range(NX):
        blk = gfr[xx]
        gin_out[:, quarter * xx : quarter * xx + quarter] = jnp.where(c == 0, blk[0:12], blk[12:24])

    @pl.when(y // 2 == c)
    def _():
        for k, (dc, dx) in enumerate(cx_peers()):
            final(k, dc, dx).wait_send()


def sum_of(buf, n):
    acc = buf[0]
    for j in range(1, n):
        acc += buf[j]
    return acc


def ordered(recv, own, t, me, n):
    acc = None
    for j in range(n):
        d = lax.rem(me - j + n, n)
        val = jnp.where(d == 0, own[t].astype(F32), recv[t, d].astype(F32))
        acc = val if acc is None else acc + val
    return acc


def on_device(
    patches, patch_view, rays, ray_view, targets, camera, slots_init, key_weight, value_weight,
    query_weight, gru_input, gru_hidden, mix_query, mix_key, render_in, render_out,
):
    n, width = patches.shape
    units = jnp.pad(render_out.T, ((0, 0), (0, 125)))
    pair = jnp.concatenate([units[0:12], units[12:24]], axis=1)
    packed = jnp.concatenate(
        [query_weight, key_weight, value_weight, mix_key, gru_input, gru_hidden, mix_query, render_in, pair], axis=1
    )
    packed = jnp.pad(packed, ((0, 4), (0, 0)))
    cam = jnp.pad(camera, ((0, 8), (0, 0)))
    V, S = pltpu.VMEM, pltpu.SemaphoreType.DMA
    vm = pl.BlockSpec(memory_space=pltpu.VMEM)
    scratch = (
        [V((128, L // NX), BF) for L in LEN]
        + [V((width, L), BF) for L in LEN]
        + [V((16, L // NX), BF) for L in LEN]
        + [
            V((16, width), BF), V((128, width), BF), V((512, width), BF),
            V((n, width), BF), V((n, width), F32), V((n, width), BF), V((8, 2 * width), BF), V((8, width), F32),
            V((3, 8, 8, width + 128), BF), V((3, 8, 8, width + 128), BF),
            V((3, 8, width + 128), BF), V((3, NY, 8, width + 128), BF),
            V((3, 8, width + 128), BF), V((3, NZ, 8, width + 128), BF),
            V((3, 8, width), BF), V((3, 8, 8, width), BF), V((8, width), F32), V((64, width), F32),
            V((8, n), F32), V((8, width), F32), V((8, 8, width), F32), V((NY, 8, width), F32), V((NZ, 8, width), F32),
            V((8, width), F32), V((8, width), F32),
            V((width, n), BF), V((384, 2 * width), F32), V((384, 2 * width), BF), V((384, 2 * width), BF),
            V((384, 2 * width), BF), V((NX, 384, width // 2), BF), V((384, width // 2), BF), V((NZ, 48, width // 2), BF),
            V((48, width // 2), F32), V((NY, 48, width // 2), F32), V((24, width // 2), F32), V((NX, 24, width // 2), F32),
            S((5, 7)), S((5, 7)), S((5, 8)), S((5, 8)), S((5, 4, 8)), S((5, 4, 8)), S((5, 8)), S((5, 8)),
            S((3, 32)), S((3, 32)), S((9, 8)), S((9, 8)),
        ]
    )
    out = pl.pallas_call(
        kernel,
        out_shape=[
            jax.ShapeDtypeStruct((64, width), F32),
            jax.ShapeDtypeStruct((3, n), F32),
            jax.ShapeDtypeStruct((1, 1), F32),
            jax.ShapeDtypeStruct((12, 2 * width), F32),
            jax.ShapeDtypeStruct((3, 2 * width), F32),
        ],
        in_specs=[vm] * 8,
        out_specs=[vm] * 5,
        scratch_shapes=scratch,
        compiler_params=pltpu.CompilerParams(collective_id=0, has_side_effects=True, vmem_limit_bytes=60 << 20),
    )(patch_view[None], ray_view[None], patches, rays, targets, slots_init, packed, cam)
    slots, colour, loss, gin, gro = out
    return slots, colour, loss[0, 0], gin, gro


def solution(mesh):
    torus = Mesh(mesh.devices.reshape(NZ, NY, NC, NX), ("z", "y", "c", "x"))
    tok, every = ("z", "y", "c"), ("z", "y", "c", "x")
    w = P(tok, None)
    return jax.shard_map(
        on_device,
        mesh=torus,
        in_specs=(
            P(every, None), P(every), P(every, None), P(every), P(None, every), w, P(),
            w, w, w, w, w, w, w, w, P(None, tok),
        ),
        out_specs=(P(), P(None, every), P(), w, P()),
        check_vma=False,
    )
```

time: 694 us -> 221 us (0.32)
  blocking collectives: 335 us -> 0 us
  Pallas kernels: 0 us -> 209 us
  waiting for transfers between devices: 166 us -> 0 us
  starting transfers between devices: 56.8 us -> 0 us
  local copies, waits for them, and re-layouts: 64.1 us -> 9.79 us
  matrix products: 41.2 us -> 0 us
  between operations: 17.9 us -> 2.48 us
  other arithmetic: 9.31 us -> 0 us
    pallas_call x0 -> x1, Pallas kernels: none -> 209 us  [on_device(): pl.pallas_call(kernel, out_shape=[jax.ShapeDtypeStruct((64, width), F32),...]
    all_to_all x9 -> x0, blocking collectives: 165 us -> none  [the longest x4 88.4 us: summed_on_arrival(): parts = lax.all_to_all(in_blocks(value, dim, size), axis, 0, 0, tiled=True)]
    all_gather x3 -> x0, waiting for transfers between devices: 126 us -> none  [the longest x2 126 us: in_one_piece(): lax.all_gather(both, axis, axis=dim, tiled=True)]
    all_gather x3 -> x0, blocking collectives: 103 us -> none  [the longest x2 52.2 us: gather_in_order(): parts = lax.all_gather(parts, axes[k], axis=0, tiled=True)]
    psum x4 -> x0, blocking collectives: 67.1 us -> none  [by_axis(): value = lax.psum(value, axis)]
    all_to_all x9 -> x0, starting transfers between devices: 56.6 us -> none  [the longest x8 48.4 us: from_everyone(): lax.all_to_all(jnp.broadcast_to(value[None], (size, *value.shape)), axis,...]
    dot_general x23 -> x0, matrix products: 41.2 us -> none  [the longest x3 8.38 us: slot_update(): jnp.dot(update.astype(jnp.bfloat16), gru_input, preferred_element_type=jn...]
    all_to_all x9 -> x0, waiting for transfers between devices: 39.3 us -> none  [the longest x8 39.3 us: from_everyone(): lax.all_to_all(jnp.broadcast_to(value[None], (size, *value.shape)), axis,...]
  transfers between devices with their start and end apart: 12 -> 0, of which waited for: 8 -> 0; matrix products, arithmetic and copies ran while one was open for 6% -> 0% of each run, Pallas kernels for 0% -> 0%
where the time goes in v1:
time: 221 us
  Pallas kernels  209 us (95%)
  local copies, waits for them, and re-layouts  9.79 us (4%)
  between operations  2.48 us (1%)
    pallas_call x1, Pallas kernels, on_device(): pl.pallas_call(kernel, out_shape=[jax.ShapeDtypeStruct((64, width), F32),...  209 us
    unnamed x36, local copies, waits for them, and re-layouts  8.41 us

profile of v1, /device:TPU:1, one launch (start us, length us, event | category | flops | bytes accessed | tf_op | source)
XLA Modules:
  0.0 220.9 jit_solution(14995691712836887300)
XLA Ops:
  0.6 0.8 copy.21
  1.4 0.0 copy-start.4
  1.4 0.0 copy-start.5
  1.4 0.8 constant_dynamic-update-slice_fusion.9
  2.2 0.0 copy-done.4
  2.2 0.0 copy-start.1
  2.2 0.0 copy-done.5
  2.2 0.0 copy-start.6
  2.2 0.7 copy-done.6
  3.0 0.1 copy-done.1
  3.0 0.0 copy-start.2
  3.1 0.9 copy-done.2
  3.9 0.0 copy-start.7
  3.9 0.7 copy-done.7
  4.7 0.0 copy-start.3
  4.7 0.8 copy-done.3
  5.5 0.0 copy-start.9
  5.5 0.8 pad.13.packed
  6.3 0.0 copy-done.9
  6.3 0.6 pad.14.camera
  6.9 208.7 %shard_map.191 = (f32[64,768]{1,0:T(8,128)}, f32[3,256]{1,0:T(4,128)}, f32[1,1]{1,0:T(1,128)}, f32[12,1536]{1,0:T(8,128)}, f32[3,1536]{1,0:T(4,128)}) custom-call(s32[1,256]{1,0:T(1,128)} %bitcast.6, s32[1,256]{1,0:T(1,128)} %bitcast.7, bf16[256,768]{1,0:T(8,128)(2,1)} %patches.1, bf16[256,768]{1,0:T(8,128)(2,1)} %rays.1, f32[3,256]{1,0:T(4,128)} %targets.1, ...), custom_call_target="tpu_custom_call" | custom-call | tf_op jit(solution)/shard_map/pallas_call | solution.py:484
  215.6 0.0 copy-start.10
  215.6 0.0 copy-start
  215.6 1.6 copy.36
  217.2 0.0 copy-done.10
  217.2 0.6 copy.37
  218.4 0.0 copy-done
  218.5 0.0 copy-start.8
  218.5 0.6 copy.39
  219.1 0.1 copy-done.8
  219.2 0.6 copy.40
  (9 shorter events, 0.1 us)
Async XLA Ops:
  1.4 0.8 copy-start.4
  1.4 0.8 copy-start.5
  2.2 0.9 copy-start.1
  2.2 0.8 copy-start.6
  3.0 0.9 copy-start.2
  3.9 0.7 copy-start.7
  4.7 0.8 copy-start.3
  5.5 0.8 copy-start.9
  215.6 1.7 copy-start.10
  215.6 2.9 %copy-start = (f32[12,1536]{1,0:T(8,128)S(1)}, f32[12,1536]{1,0:T(8,128)}, u32[]{:S(2)}) copy-start(f32[12,1536]{1,0:T(8,128)} %get-tuple-element.23) | copy-start | bytes 221188
  218.5 0.7 copy-start.8

commit v2 on v1

--- a/solution.py
+++ b/solution.py
@@ -97,92 +97,121 @@
     pl.semaphore_wait(barrier, met)
 
     me_yc = y * 2 + c
-
-    def start_yc(src, buf, slot):
-        buf[rows(me_yc * 16, 16), :] = src[...]
+    quarter = x * (1 - c) + y * c
+
+    def along(d):
+        return dict(x=lax.rem(x + d * (1 - c), NX), y=lax.rem(y + d * c, NY))
+
+    def across(d):
+        return dict(x=lax.rem(x + d * c, NX), y=lax.rem(y + d * (1 - c), NY))
+
+    def yc_copies(src, buf, slot, w, part):
         out = []
         for k, (dy, dc) in enumerate(yc_peers()):
-            out.append(send(src, buf.at[rows(me_yc * 16, 16)], cy_s.at[slot, k], cy_r.at[slot, k],
-                            y=lax.rem(y + dy, NY), c=flip(dc)))
+            yy, cc = lax.rem(y + dy, NY), flip(dc)
+            cp = pltpu.make_async_remote_copy(
+                src_ref=src.at[:, lanes(part(yy, cc) * w, w)], dst_ref=buf.at[rows(me_yc * 16, 16)],
+                send_sem=cy_s.at[slot, k], recv_sem=cy_r.at[slot, k],
+                device_id={"y": yy, "c": cc}, device_id_type=pl.DeviceIdType.MESH,
+            )
+            out.append((cp, dy, cc))
         return out
 
     def start_bundle(b):
         w = LEN[b] // NX
-        stage[b][...] = packed[:, lanes(OFF[b] + x * w, w)]
-        return start_yc(stage[b], cyb[b], b)
+        stage[b][...] = packed[:, OFF[b] : OFF[b] + LEN[b]]
+        cyb[b][rows(me_yc * 16, 16), :] = stage[b][:, lanes(quarter * w, w)]
+        cps = yc_copies(stage[b], cyb[b], b, w, lambda yy, cc: x * (1 - cc) + yy * cc)
+        for cp, dy, cc in cps:
+            @pl.when(y // 2 == cc)
+            def _():
+                cp.start()
+
+        return cps
+
+    def finish_bundle(cps):
+        for cp, dy, cc in cps:
+            @pl.when(lax.rem(y - dy + NY, NY) // 2 == c)
+            def _():
+                cp.wait_recv()
+
+            @pl.when(y // 2 == cc)
+            def _():
+                cp.wait_send()
 
     def compact(shards, real, first, count):
-        r = lax.broadcasted_iota(jnp.int32, (count, 128), 0) + first
-        k = lax.broadcasted_iota(jnp.int32, (count, 128), 1)
+        n = shards.shape[0]
+        r = lax.broadcasted_iota(jnp.int32, (count, n), 0) + first
+        k = lax.broadcasted_iota(jnp.int32, (count, n), 1)
         lane = k % 16
         mask = (lane < real) & (r == (k // 16) * real + lane)
         return dot(onehot(mask), shards).astype(BF)
 
     def piece(b, zz):
         w = LEN[b] // NX
-        return full[b].at[rows(zz * 96 + c * 48, 48), lanes(x * w, w)]
+        return full[b].at[rows(zz * 96 + c * 48, 48), lanes(quarter * w, w)]
 
     def start_z(b, arrived):
-        for cp in arrived:
-            cp.wait()
+        finish_bundle(arrived)
         w = LEN[b] // NX
-        full[b][rows(z * 96 + c * 48, 48), lanes(x * w, w)] = compact(cyb[b][...], 12, c * 48, 48)
+        full[b][rows(z * 96 + c * 48, 48), lanes(quarter * w, w)] = compact(cyb[b][rows(c * 64, 64), :], 12, 0, 48)
         return [
             send(piece(b, z), piece(b, z), z_s.at[b, d], z_r.at[b, d], z=lax.rem(z + d, NZ))
             for d in range(1, NZ)
         ]
 
     def forward_x(b, ref, d):
-        return [
-            send(ref, ref, x_s.at[b, dx, d], x_r.at[b, dx, d], x=lax.rem(x + dx, NX))
-            for dx in range(1, NX)
-        ]
+        return [send(ref, ref, x_s.at[b, k, d], x_r.at[b, k, d], **along(k)) for k in range(1, NX)]
 
     def start_x(b, arriving):
-        out = forward_x(b, piece(b, z), 0)
+        out = [forward_x(b, piece(b, z), 0)]
         for d in range(1, NZ):
             arriving[d - 1].wait()
-            out += forward_x(b, piece(b, lax.rem(z - d + NZ, NZ)), d)
+            out.append(forward_x(b, piece(b, lax.rem(z - d + NZ, NZ)), d))
         return out
 
     def swap_core(b, arriving):
-        for cp in arriving:
-            cp.wait()
         cps = []
-        for zz in range(NZ):
-            ref = full[b].at[rows(zz * 96 + c * 48, 48)]
-            cps.append(send(ref, ref, c_s.at[b, zz], c_r.at[b, zz], c=1 - c))
+        for d in range(NZ):
+            for cp in arriving[d]:
+                cp.wait()
+            ref = full[b].at[rows(lax.rem(z - d + NZ, NZ) * 96 + c * 48, 48)]
+            cps.append(send(ref, ref, c_s.at[b, d], c_r.at[b, d], c=1 - c))
         return cps
 
     def done(cps):
         for cp in cps:
             cp.wait()
 
+    half = width // 2
     cy_b0 = start_bundle(0)
     camsg[...] = camera[...]
-    cy_cam = start_yc(camsg, camcy, 4)
+    camcy[rows(me_yc * 16, 16), :] = camsg[:, lanes(c * half, half)]
+    cy_cam = yc_copies(camsg, camcy, 4, half, lambda yy, cc: cc)
+    for cp, _, _ in cy_cam:
+        cp.start()
     n0 = normalize(slots_init[...]).astype(BF)
     z_b0 = start_z(0, cy_b0)
-    done(cy_cam)
-    half = width // 2
-    camf[rows(z * 64 + x * 16, 16), lanes(c * half, half)] = compact(camcy[:, lanes(c * half, half)], 8, x * 16, 16)
+    for cp, _, _ in cy_cam:
+        cp.wait()
+    camf[rows(z * 64 + quarter * 16, 16), lanes(c * half, half)] = compact(camcy[...], 8, quarter * 16, 16)
 
     def cam_piece(zz):
-        return camf.at[rows(zz * 64 + x * 16, 16), lanes(c * half, half)]
+        return camf.at[rows(zz * 64 + quarter * 16, 16), lanes(c * half, half)]
 
     z_cam = [
         send(cam_piece(z), cam_piece(z), z_s.at[4, d], z_r.at[4, d], z=lax.rem(z + d, NZ))
         for d in range(1, NZ)
     ]
+    cy_b1 = start_bundle(1)
     cy_b2 = start_bundle(2)
-    cy_b1 = start_bundle(1)
     x_cam = forward_x(4, cam_piece(z), 0)
     for d in range(1, NZ):
         z_cam[d - 1].wait()
         x_cam += forward_x(4, cam_piece(lax.rem(z - d + NZ, NZ)), d)
     x_b0 = start_x(0, z_b0)
+    z_b1 = start_z(1, cy_b1)
     z_b2 = start_z(2, cy_b2)
-    z_b1 = start_z(1, cy_b1)
     done(x_cam)
     cam_half = camf.at[:, lanes(c * half, half)]
     done([send(cam_half, cam_half, c_s.at[4, 0], c_r.at[4, 0], c=1 - c)])
@@ -336,9 +365,9 @@
     g_c.wait()
     gown[...] += gcr[...].astype(F32)
     gxs[...] = gown[...].astype(BF)
-    quarter = 2 * width // NX
+    qw = 2 * width // NX
     gx = [
-        send(gxs.at[:, lanes(lax.rem(x + d, NX) * quarter, quarter)], gxr.at[d], gr_s.at[3, d], gr_r.at[3, d], x=lax.rem(x + d, NX))
+        send(gxs.at[:, lanes(lax.rem(quarter + d, NX) * qw, qw)], gxr.at[d], gr_s.at[3, d], gr_r.at[3, d], **along(d))
         for d in range(1, NX)
     ]
     done(sm_cps)
@@ -355,7 +384,7 @@
     sm_cps = [
         send(smz, smrecv_z.at[z], gr_s.at[5, d], gr_r.at[5, d], z=lax.rem(z + d, NZ)) for d in range(1, NZ)
     ]
-    acc_g = gown[:, lanes(x * quarter, quarter)]
+    acc_g = gown[:, lanes(quarter * qw, qw)]
     for d, cp in enumerate(gx):
         cp.wait()
         acc_g += gxr[d + 1].astype(F32)
@@ -373,62 +402,62 @@
     for d, cp in enumerate(gz):
         cp.wait()
         acc_g += gzr[d + 1].astype(F32)
-    gys[...] = acc_g
-    for d in range(1, NY):
-        to = lax.rem(y + d, NY)
-
-        @pl.when(to // 2 == c)
+    gys[0] = acc_g.astype(BF)
+    for cp in [send(gys.at[0], gyr.at[0, d], gr_s.at[7, d], gr_r.at[7, d], **across(d)) for d in range(1, NY)]:
+        cp.wait()
+    place = x * c + y * (1 - c)
+    gfs[...] = ordered(gyr, gys, 0, place, NY)
+
+    def final(k, row, slot, **where):
+        return pltpu.make_async_remote_copy(
+            src_ref=gfs.at[pl.ds(pl.multiple_of(row * 24, 8), 24)], dst_ref=gfr.at[slot],
+            send_sem=gr_s.at[8, k], recv_sem=gr_r.at[8, slot],
+            device_id=where, device_id_type=pl.DeviceIdType.MESH,
+        )
+
+    low_half = y // 2 == 0
+    keeps = y // 2 == c
+    own_row = lax.rem(y, 2)
+
+    @pl.when(keeps)
+    def _():
+        gfr[quarter] = gfs[pl.ds(pl.multiple_of(own_row * 24, 8), 24), :]
+
+    def to_x(act):
+        for k, (dc, dx) in enumerate(cx_peers()):
+            act(final(k, own_row, quarter, c=flip(dc), x=lax.rem(x + dx, NX)))
+
+    def to_y(act):
+        for k in range(4):
+            yy, cc = 2 + k // 2, k % 2
+
+            @pl.when(jnp.logical_not((y == yy) & (c == cc)))
+            def _():
+                act(final(k, k // 2, quarter, y=yy, c=cc))
+
+    @pl.when((c == 0) & low_half)
+    def _():
+        to_x(lambda cp: cp.start())
+
+    @pl.when(c == 1)
+    def _():
+        to_y(lambda cp: cp.start())
+
+    for slot in range(NX):
+        @pl.when(jnp.logical_not(keeps & (quarter == slot)))
         def _():
-            pltpu.make_async_remote_copy(
-                src_ref=gys, dst_ref=gyr.at[d], send_sem=gr_s.at[7, d], recv_sem=gr_r.at[7, d],
-                device_id={"y": to}, device_id_type=pl.DeviceIdType.MESH,
-            ).start()
-
-    def final(k, dc, dx):
-        return pltpu.make_async_remote_copy(
-            src_ref=gfs, dst_ref=gfr.at[x], send_sem=gr_s.at[8, k], recv_sem=gr_r.at[8, dx],
-            device_id={"c": flip(dc), "x": lax.rem(x + dx, NX)}, device_id_type=pl.DeviceIdType.MESH,
-        )
-
-    @pl.when(y // 2 == c)
+            final(0, 0, slot, c=1 - c).wait_recv()
+
+        blk = gfr[slot]
+        gin_out[:, qw * slot : qw * slot + qw] = jnp.where(c == 0, blk[0:12], blk[12:24])
+
+    @pl.when((c == 0) & low_half)
     def _():
-        acc = gys[...]
-        for d in range(1, NY):
-            pltpu.make_async_remote_copy(
-                src_ref=gys, dst_ref=gyr.at[d], send_sem=gr_s.at[7, d], recv_sem=gr_r.at[7, d],
-                device_id={"y": lax.rem(y + d, NY)}, device_id_type=pl.DeviceIdType.MESH,
-            ).wait_recv()
-            acc += gyr[d]
-        part = jnp.where(y % 2 == 0, acc[0:24], acc[24:48])
-        gfs[...] = part
-        gfr[x] = part
-        for k, (dc, dx) in enumerate(cx_peers()):
-            final(k, dc, dx).start()
-
-    for d in range(1, NY):
-        to = lax.rem(y + d, NY)
-
-        @pl.when(to // 2 == c)
-        def _():
-            pltpu.make_async_remote_copy(
-                src_ref=gys, dst_ref=gyr.at[d], send_sem=gr_s.at[7, d], recv_sem=gr_r.at[7, d],
-                device_id={"y": to}, device_id_type=pl.DeviceIdType.MESH,
-            ).wait_send()
-
-    @pl.when(y // 2 != c)
+        to_x(lambda cp: cp.wait_send())
+
+    @pl.when(c == 1)
     def _():
-        final(0, 0, 0).wait_recv()
-
-    for dx in range(1, NX):
-        final(0, 0, dx).wait_recv()
-    for xx in range(NX):
-        blk = gfr[xx]
-        gin_out[:, quarter * xx : quarter * xx + quarter] = jnp.where(c == 0, blk[0:12], blk[12:24])
-
-    @pl.when(y // 2 == c)
-    def _():
-        for k, (dc, dx) in enumerate(cx_peers()):
-            final(k, dc, dx).wait_send()
+        to_y(lambda cp: cp.wait_send())
 
 
 def sum_of(buf, n):
@@ -464,9 +493,9 @@
     scratch = (
         [V((128, L // NX), BF) for L in LEN]
         + [V((width, L), BF) for L in LEN]
-        + [V((16, L // NX), BF) for L in LEN]
+        + [V((16, L), BF) for L in LEN]
         + [
-            V((16, width), BF), V((128, width), BF), V((512, width), BF),
+            V((16, width), BF), V((128, width // 2), BF), V((512, width), BF),
             V((n, width), BF), V((n, width), F32), V((n, width), BF), V((8, 2 * width), BF), V((8, width), F32),
             V((3, 8, 8, width + 128), BF), V((3, 8, 8, width + 128), BF),
             V((3, 8, width + 128), BF), V((3, NY, 8, width + 128), BF),
@@ -476,7 +505,7 @@
             V((8, width), F32), V((8, width), F32),
             V((width, n), BF), V((384, 2 * width), F32), V((384, 2 * width), BF), V((384, 2 * width), BF),
             V((384, 2 * width), BF), V((NX, 384, width // 2), BF), V((384, width // 2), BF), V((NZ, 48, width // 2), BF),
-            V((48, width // 2), F32), V((NY, 48, width // 2), F32), V((24, width // 2), F32), V((NX, 24, width // 2), F32),
+            V((1, 48, width // 2), BF), V((1, NY, 48, width // 2), BF), V((48, width // 2), F32), V((NX, 24, width // 2), F32),
             S((5, 7)), S((5, 7)), S((5, 8)), S((5, 8)), S((5, 4, 8)), S((5, 4, 8)), S((5, 8)), S((5, 8)),
             S((3, 32)), S((3, 32)), S((9, 8)), S((9, 8)),
         ]

time: 221 us -> 183 us (0.83)
  Pallas kernels: 209 us -> 171 us
    pallas_call x1, Pallas kernels: 209 us -> 171 us  [on_device(): pl.pallas_call(kernel, out_shape=[jax.ShapeDtypeStruct((64, width), F32),...]
where the time goes in v2:
time: 183 us
  Pallas kernels  171 us (93%)
  local copies, waits for them, and re-layouts  9.79 us (5%)
  between operations  2.48 us (1%)
    pallas_call x1, Pallas kernels, on_device(): pl.pallas_call(kernel, out_shape=[jax.ShapeDtypeStruct((64, width), F32),...  171 us
    unnamed x36, local copies, waits for them, and re-layouts  8.41 us

profile of v2, /device:TPU:1, one launch (start us, length us, event | category | flops | bytes accessed | tf_op | source)
XLA Modules:
  0.0 182.9 jit_solution(5009868918396376376)
XLA Ops:
  0.6 0.8 copy.21
  1.4 0.0 copy-start.4
  1.4 0.0 copy-start.5
  1.4 0.8 constant_dynamic-update-slice_fusion.9
  2.2 0.0 copy-done.4
  2.2 0.0 copy-start.1
  2.2 0.0 copy-done.5
  2.2 0.0 copy-start.6
  2.2 0.7 copy-done.6
  3.0 0.1 copy-done.1
  3.0 0.0 copy-start.2
  3.1 0.9 copy-done.2
  3.9 0.0 copy-start.7
  3.9 0.7 copy-done.7
  4.7 0.0 copy-start.3
  4.7 0.8 copy-done.3
  5.5 0.0 copy-start.9
  5.5 0.8 pad.13.packed
  6.3 0.0 copy-done.9
  6.3 0.6 pad.14.camera
  6.9 170.7 %shard_map.191 = (f32[64,768]{1,0:T(8,128)}, f32[3,256]{1,0:T(4,128)}, f32[1,1]{1,0:T(1,128)}, f32[12,1536]{1,0:T(8,128)}, f32[3,1536]{1,0:T(4,128)}) custom-call(s32[1,256]{1,0:T(1,128)} %bitcast.6, s32[1,256]{1,0:T(1,128)} %bitcast.7, bf16[256,768]{1,0:T(8,128)(2,1)} %patches.1, bf16[256,768]{1,0:T(8,128)(2,1)} %rays.1, f32[3,256]{1,0:T(4,128)} %targets.1, ...), custom_call_target="tpu_custom_call" | custom-call | tf_op jit(solution)/shard_map/pallas_call | solution.py:513
  177.6 0.0 copy-start.10
  177.6 0.0 copy-start
  177.6 1.6 copy.36
  179.2 0.0 copy-done.10
  179.2 0.6 copy.37
  180.5 0.0 copy-done
  180.5 0.0 copy-start.8
  180.5 0.6 copy.39
  181.1 0.1 copy-done.8
  181.2 0.6 copy.40
  (9 shorter events, 0.1 us)
Async XLA Ops:
  1.4 0.8 copy-start.4
  1.4 0.8 copy-start.5
  2.2 0.9 copy-start.1
  2.2 0.8 copy-start.6
  3.0 0.9 copy-start.2
  3.9 0.7 copy-start.7
  4.7 0.8 copy-start.3
  5.5 0.8 copy-start.9
  177.6 1.7 copy-start.10
  177.6 2.9 %copy-start = (f32[12,1536]{1,0:T(8,128)S(1)}, f32[12,1536]{1,0:T(8,128)}, u32[]{:S(2)}) copy-start(f32[12,1536]{1,0:T(8,128)} %get-tuple-element.23) | copy-start | bytes 221188
  180.5 0.7 copy-start.8

commit v3 on v2

--- a/solution.py
+++ b/solution.py
@@ -15,7 +15,6 @@
 BF = jnp.bfloat16
 F32 = jnp.float32
 
-OFF = (0, 1536, 3072, 7680)
 LEN = (1536, 1536, 4608, 2560)
 NB = 4
 
@@ -50,9 +49,10 @@
 
 
 def kernel(
-    pview, rview, patches, rays, targets, slots_init, packed, camera,
+    pview, rview, patches, rays, targets, slots_init, camera,
+    wq, wk, wv, mk, gi, gh, mq, rin_w, rout,
     slots_out, colour_out, loss_out, gin_out, gro_out,
-    cy0, cy1, cy2, cy3, f0, f1, f2, f3, sg0, sg1, sg2, sg3, camsg, camcy, camf,
+    cy0, cy1, cy2, cy3, f0, f1, f2, f3, sg0, sg1, sg2, sg3, rp, camsg, camcy, camf,
     px, rin, rx, ro, state, tsend, trecv, tysend, tyrecv, tzsend, tzrecv,
     psend, precv, ssend, srecv, dcol8, small, smrecv_cx, smrecv_y, smrecv_z, smy, smz,
     jt, gown, gcs, gcr, gxs, gxr, gzs, gzr, gys, gyr, gfs, gfr,
@@ -117,9 +117,24 @@
             out.append((cp, dy, cc))
         return out
 
+    def pack(b, parts):
+        stage[b][...] = jnp.zeros_like(stage[b])
+        at = 0
+        for part in parts:
+            stage[b][0:12, at : at + part.shape[1]] = part[...]
+            at += part.shape[1]
+
+    def pack_colour(at):
+        rp[...] = jnp.zeros_like(rp)
+        rp[0:3, :] = rout[...].astype(F32)
+        unit = lax.broadcasted_iota(jnp.int32, (16, 24), 1)
+        row = lax.broadcasted_iota(jnp.int32, (16, 24), 0)
+        for j in range(2):
+            mask = (unit == row + 12 * j) & (row < 12)
+            stage[3][:, at + 128 * j : at + 128 * j + 128] = dot(onehot(mask), rp[...].astype(BF), 1, 1).astype(BF)
+
     def start_bundle(b):
         w = LEN[b] // NX
-        stage[b][...] = packed[:, OFF[b] : OFF[b] + LEN[b]]
         cyb[b][rows(me_yc * 16, 16), :] = stage[b][:, lanes(quarter * w, w)]
         cps = yc_copies(stage[b], cyb[b], b, w, lambda yy, cc: x * (1 - cc) + yy * cc)
         for cp, dy, cc in cps:
@@ -151,29 +166,56 @@
         w = LEN[b] // NX
         return full[b].at[rows(zz * 96 + c * 48, 48), lanes(quarter * w, w)]
 
-    def start_z(b, arrived):
+    def start_z(b, arrived, ring=True):
         finish_bundle(arrived)
         w = LEN[b] // NX
         full[b][rows(z * 96 + c * 48, 48), lanes(quarter * w, w)] = compact(cyb[b][rows(c * 64, 64), :], 12, 0, 48)
-        return [
-            send(piece(b, z), piece(b, z), z_s.at[b, d], z_r.at[b, d], z=lax.rem(z + d, NZ))
-            for d in range(1, NZ)
-        ]
+        if not ring:
+            return [
+                send(piece(b, z), piece(b, z), z_s.at[b, d], z_r.at[b, d], z=lax.rem(z + d, NZ))
+                for d in range(1, NZ)
+            ]
+        return [pass_on(b, z, 1), pass_on(b, z, NZ - 1)]
+
+    def pass_on(b, zz, d):
+        to = lax.rem(z + (1 if d <= NZ // 2 else NZ - 1), NZ)
+        return send(piece(b, zz), piece(b, zz), z_s.at[b, d], z_r.at[b, d], z=to)
 
     def forward_x(b, ref, d):
         return [send(ref, ref, x_s.at[b, k, d], x_r.at[b, k, d], **along(k)) for k in range(1, NX)]
 
     def start_x(b, arriving):
-        out = [forward_x(b, piece(b, z), 0)]
+        out = [(0, forward_x(b, piece(b, z), 0))]
         for d in range(1, NZ):
             arriving[d - 1].wait()
-            out.append(forward_x(b, piece(b, lax.rem(z - d + NZ, NZ)), d))
-        return out
-
-    def swap_core(b, arriving):
+            out.append((d, forward_x(b, piece(b, lax.rem(z - d + NZ, NZ)), d)))
+        return out, []
+
+    def ring_x(bundles):
+        out = {b: [(0, forward_x(b, piece(b, z), 0))] for b, _ in bundles}
+        sent = {b: list(first) for b, first in bundles}
+        for k in range(1, NZ // 2 + 1):
+            for d in (k, NZ - k) if k < NZ // 2 else (k,):
+                for b, _ in bundles:
+                    zz = lax.rem(z - d + NZ, NZ)
+                    pltpu.make_async_remote_copy(
+                        src_ref=piece(b, zz), dst_ref=piece(b, zz), send_sem=z_s.at[b, d], recv_sem=z_r.at[b, d],
+                        device_id={"z": zz}, device_id_type=pl.DeviceIdType.MESH,
+                    ).wait_recv()
+                    if d < NZ // 2:
+                        sent[b].append(pass_on(b, zz, d + 1))
+                    if d > NZ // 2 + 1:
+                        sent[b].append(pass_on(b, zz, d - 1))
+                    out[b].append((d, forward_x(b, piece(b, zz), d)))
+        return {b: (out[b], sent[b]) for b, _ in bundles}
+
+    def swap_core(b, gathered):
+        arriving, sent = gathered
+        for cp in sent:
+            cp.wait_send()
         cps = []
-        for d in range(NZ):
-            for cp in arriving[d]:
+        for d, group_cps in arriving:
+            for cp in group_cps:
                 cp.wait()
             ref = full[b].at[rows(lax.rem(z - d + NZ, NZ) * 96 + c * 48, 48)]
             cps.append(send(ref, ref, c_s.at[b, d], c_r.at[b, d], c=1 - c))
@@ -184,8 +226,10 @@
             cp.wait()
 
     half = width // 2
+    pack(0, (wq, wk))
     cy_b0 = start_bundle(0)
-    camsg[...] = camera[...]
+    camsg[...] = jnp.zeros_like(camsg)
+    camsg[0:8, :] = camera[...]
     camcy[rows(me_yc * 16, 16), :] = camsg[:, lanes(c * half, half)]
     cy_cam = yc_copies(camsg, camcy, 4, half, lambda yy, cc: cc)
     for cp, _, _ in cy_cam:
@@ -203,15 +247,23 @@
         send(cam_piece(z), cam_piece(z), z_s.at[4, d], z_r.at[4, d], z=lax.rem(z + d, NZ))
         for d in range(1, NZ)
     ]
+    pack(1, (wv, mk))
     cy_b1 = start_bundle(1)
+    pack(2, (gi, gh))
     cy_b2 = start_bundle(2)
+    x_b0 = ring_x([(0, z_b0)])[0]
+    z_b1 = start_z(1, cy_b1)
+    z_b2 = start_z(2, cy_b2)
     x_cam = forward_x(4, cam_piece(z), 0)
     for d in range(1, NZ):
         z_cam[d - 1].wait()
         x_cam += forward_x(4, cam_piece(lax.rem(z - d + NZ, NZ)), d)
-    x_b0 = start_x(0, z_b0)
-    z_b1 = start_z(1, cy_b1)
-    z_b2 = start_z(2, cy_b2)
+    pack(3, (mq, rin_w))
+    pack_colour(3 * width)
+    cy_b3 = start_bundle(3)
+    c_b0 = swap_core(0, x_b0)
+    bulk = ring_x([(1, z_b1), (2, z_b2)])
+    z_b3 = start_z(3, cy_b3, ring=False)
     done(x_cam)
     cam_half = camf.at[:, lanes(c * half, half)]
     done([send(cam_half, cam_half, c_s.at[4, 0], c_r.at[4, 0], c=1 - c)])
@@ -223,7 +275,7 @@
     px[...] = normalize(patches[...].astype(F32) + lookup(pview)).astype(BF)
     rin[...] = rays[...].astype(F32) + lookup(rview)
     rx[...] = rin[...].astype(BF)
-    done(swap_core(0, x_b0))
+    done(c_b0)
 
     def slot_projection(normed):
         query = (dot(normed, f0[:, 0:width]) * scale).astype(BF)
@@ -233,7 +285,7 @@
     mine = pl.ds(pl.multiple_of(group * 8, 8), 8)
     state[...] = slots_init[mine, :]
     proj = slot_projection(n0)
-    x_b1 = x_b2 = x_b3 = cy_b3 = z_b3 = c_b3 = None
+    x_b3 = c_b3 = None
 
     def group_rows(buf, t):
         return jnp.concatenate([buf[t, g].astype(F32) for g in range(8)], axis=0)
@@ -258,14 +310,6 @@
         for k, (dc, dx) in enumerate(cx_peers()):
             cc, xx = flip(dc), lax.rem(x + dx, NX)
             cps.append(send(tsend.at[t, cc * NX + xx], trecv.at[t, k], it_s.at[t, k], it_r.at[t, k], c=cc, x=xx))
-        if t == 0:
-            x_b1 = start_x(1, z_b1)
-            x_b2 = start_x(2, z_b2)
-            cy_b3 = start_bundle(3)
-        if t == 1:
-            x_b3 = start_x(3, z_b3)
-        if t == 2:
-            c_b3 = swap_core(3, x_b3)
         acc = tsend[t, group].astype(F32)
         for k, cp in enumerate(cps):
             cp.wait()
@@ -284,13 +328,15 @@
             for d in range(1, NZ)
         ]
         if t == 0:
-            c_b1 = swap_core(1, x_b1)
-            c_b2 = swap_core(2, x_b2)
-            z_b3 = start_z(3, cy_b3)
+            c_b1 = swap_core(1, bulk[1])
+            c_b2 = swap_core(2, bulk[2])
+        if t == 1:
+            c_b3 = swap_core(3, x_b3)
         for cp in cps:
             cp.wait()
         acc = ordered(tzrecv, tzsend, t, z, NZ)
         if t == 0:
+            x_b3 = start_x(3, z_b3)
             done(c_b1)
             done(c_b2)
         mean_x = (acc[:, 0:width] / acc[:, width : width + 1]).astype(BF)
@@ -481,13 +527,6 @@
     query_weight, gru_input, gru_hidden, mix_query, mix_key, render_in, render_out,
 ):
     n, width = patches.shape
-    units = jnp.pad(render_out.T, ((0, 0), (0, 125)))
-    pair = jnp.concatenate([units[0:12], units[12:24]], axis=1)
-    packed = jnp.concatenate(
-        [query_weight, key_weight, value_weight, mix_key, gru_input, gru_hidden, mix_query, render_in, pair], axis=1
-    )
-    packed = jnp.pad(packed, ((0, 4), (0, 0)))
-    cam = jnp.pad(camera, ((0, 8), (0, 0)))
     V, S = pltpu.VMEM, pltpu.SemaphoreType.DMA
     vm = pl.BlockSpec(memory_space=pltpu.VMEM)
     scratch = (
@@ -495,7 +534,7 @@
         + [V((width, L), BF) for L in LEN]
         + [V((16, L), BF) for L in LEN]
         + [
-            V((16, width), BF), V((128, width // 2), BF), V((512, width), BF),
+            V((128, 24), F32), V((16, width), BF), V((128, width // 2), BF), V((512, width), BF),
             V((n, width), BF), V((n, width), F32), V((n, width), BF), V((8, 2 * width), BF), V((8, width), F32),
             V((3, 8, 8, width + 128), BF), V((3, 8, 8, width + 128), BF),
             V((3, 8, width + 128), BF), V((3, NY, 8, width + 128), BF),
@@ -519,11 +558,14 @@
             jax.ShapeDtypeStruct((12, 2 * width), F32),
             jax.ShapeDtypeStruct((3, 2 * width), F32),
         ],
-        in_specs=[vm] * 8,
+        in_specs=[vm] * 16,
         out_specs=[vm] * 5,
         scratch_shapes=scratch,
         compiler_params=pltpu.CompilerParams(collective_id=0, has_side_effects=True, vmem_limit_bytes=60 << 20),
-    )(patch_view[None], ray_view[None], patches, rays, targets, slots_init, packed, cam)
+    )(
+        patch_view[None], ray_view[None], patches, rays, targets, slots_init, camera, query_weight, key_weight,
+        value_weight, mix_key, gru_input, gru_hidden, mix_query, render_in, render_out,
+    )
     slots, colour, loss, gin, gro = out
     return slots, colour, loss[0, 0], gin, gro
 

time: 183 us -> 174 us (0.951)
  local copies, waits for them, and re-layouts: 9.79 us -> 3.59 us
  Pallas kernels: 171 us -> 168 us
    unnamed x36 -> x10, local copies, waits for them, and re-layouts: 8.41 us -> 3.59 us
    pallas_call x1, Pallas kernels: 171 us -> 168 us  [on_device(): pl.pallas_call(kernel, out_shape=[jax.ShapeDtypeStruct((64, width), F32),...]
where the time goes in v3:
time: 174 us
  Pallas kernels  168 us (97%)
  local copies, waits for them, and re-layouts  3.59 us (2%)
  between operations  2.44 us (1%)
    pallas_call x1, Pallas kernels, on_device(): pl.pallas_call(kernel, out_shape=[jax.ShapeDtypeStruct((64, width), F32),...  168 us
    unnamed x10, local copies, waits for them, and re-layouts  3.59 us

profile of v3, /device:TPU:1, one launch (start us, length us, event | category | flops | bytes accessed | tf_op | source)
XLA Modules:
  0.0 174.2 jit_solution(17124636221551348782)
XLA Ops:
  0.6 168.1 %shard_map.191 = (f32[64,768]{1,0:T(8,128)}, f32[3,256]{1,0:T(4,128)}, f32[1,1]{1,0:T(1,128)}, f32[12,1536]{1,0:T(8,128)}, f32[3,1536]{1,0:T(4,128)}) custom-call(s32[1,256]{1,0:T(1,128)} %bitcast.3, s32[1,256]{1,0:T(1,128)} %bitcast.4, bf16[256,768]{1,0:T(8,128)(2,1)} %patches.1, bf16[256,768]{1,0:T(8,128)(2,1)} %rays.1, f32[3,256]{1,0:T(4,128)} %targets.1, ...), custom_call_target="tpu_custom_call" | custom-call | tf_op jit(solution)/shard_map/pallas_call | solution.py:552
  168.8 0.0 copy-start.2
  168.8 0.0 copy-start
  168.8 1.6 copy.26
  170.5 0.0 copy-done.2
  170.5 0.6 copy.27
  171.7 0.0 copy-done
  171.7 0.0 copy-start.1
  171.7 0.6 copy.29
  172.3 0.1 copy-done.1
  172.4 0.6 copy.30
Async XLA Ops:
  168.8 1.7 copy-start.2
  168.8 2.9 %copy-start = (f32[12,1536]{1,0:T(8,128)S(1)}, f32[12,1536]{1,0:T(8,128)}, u32[]{:S(2)}) copy-start(f32[12,1536]{1,0:T(8,128)} %get-tuple-element.23) | copy-start | bytes 221188
  171.7 0.7 copy-start.1

commit v4 on v3

--- a/solution.py
+++ b/solution.py
@@ -56,7 +56,7 @@
     px, rin, rx, ro, state, tsend, trecv, tysend, tyrecv, tzsend, tzrecv,
     psend, precv, ssend, srecv, dcol8, small, smrecv_cx, smrecv_y, smrecv_z, smy, smz,
     jt, gown, gcs, gcr, gxs, gxr, gzs, gzr, gys, gyr, gfs, gfr,
-    cy_s, cy_r, z_s, z_r, x_s, x_r, c_s, c_r, it_s, it_r, gr_s, gr_r,
+    cy_s, cy_r, z_s, z_r, x_s, x_r, c_s, c_r, it_s, it_r, gr_s, gr_r, gc_s, gc_r, gx_s, gx_r,
 ):
     z, y, c, x = (lax.axis_index(a) for a in ("z", "y", "c", "x"))
     cyb, full, stage = (cy0, cy1, cy2, cy3), (f0, f1, f2, f3), (sg0, sg1, sg2, sg3)
@@ -183,13 +183,6 @@
 
     def forward_x(b, ref, d):
         return [send(ref, ref, x_s.at[b, k, d], x_r.at[b, k, d], **along(k)) for k in range(1, NX)]
-
-    def start_x(b, arriving):
-        out = [(0, forward_x(b, piece(b, z), 0))]
-        for d in range(1, NZ):
-            arriving[d - 1].wait()
-            out.append((d, forward_x(b, piece(b, lax.rem(z - d + NZ, NZ)), d)))
-        return out, []
 
     def ring_x(bundles):
         out = {b: [(0, forward_x(b, piece(b, z), 0))] for b, _ in bundles}
@@ -285,7 +278,8 @@
     mine = pl.ds(pl.multiple_of(group * 8, 8), 8)
     state[...] = slots_init[mine, :]
     proj = slot_projection(n0)
-    x_b3 = c_b3 = None
+    x_b3, c_b3 = [], []
+    gaps = ((0, 1, 2), (3, 4, 5), (6, 7))
 
     def group_rows(buf, t):
         return jnp.concatenate([buf[t, g].astype(F32) for g in range(8)], axis=0)
@@ -330,13 +324,17 @@
         if t == 0:
             c_b1 = swap_core(1, bulk[1])
             c_b2 = swap_core(2, bulk[2])
-        if t == 1:
-            c_b3 = swap_core(3, x_b3)
+        if t:
+            c_b3 += swap_core(3, (x_b3, []))
+            x_b3 = []
+        for d in gaps[t]:
+            if d:
+                z_b3[d - 1].wait()
+            x_b3.append((d, forward_x(3, piece(3, lax.rem(z - d + NZ, NZ)), d)))
         for cp in cps:
             cp.wait()
         acc = ordered(tzrecv, tzsend, t, z, NZ)
         if t == 0:
-            x_b3 = start_x(3, z_b3)
             done(c_b1)
             done(c_b2)
         mean_x = (acc[:, 0:width] / acc[:, width : width + 1]).astype(BF)
@@ -361,7 +359,7 @@
         send(ssend, srecv.at[mine], gr_s.at[0, k], gr_r.at[0, k], c=flip(dc), x=lax.rem(x + dx, NX))
         for k, (dc, dx) in enumerate(cx_peers())
     ]
-    done(c_b3)
+    done(c_b3 + swap_core(3, (x_b3, [])))
     slot_keys = dot(slots.astype(BF), f1[:, width : 2 * width]).astype(BF)
     r_cps = share(t, (dot(slot_keys, f3[:, 0:width], 1, 1) * scale).astype(BF))
     r = lax.broadcasted_iota(jnp.int32, (width, 1), 0)
@@ -396,8 +394,13 @@
     for zz in range(NZ):
         for h in range(NC):
             jt[384 * h + 48 * zz : 384 * h + 48 * zz + 48, :] = turned[96 * zz + 48 * h : 96 * zz + 48 * h + 48]
+    order = (4, 3, 5, 2, 6, 1, 7, 0)
+
+    def block(d):
+        return rows(lax.rem(z + d, NZ) * 48, 48)
+
     gcs[...] = dot(jt[rows(384 * (1 - c), 384), :], dpre).astype(BF)
-    g_c = send(gcs, gcr, gr_s.at[1, 0], gr_r.at[1, 0], c=1 - c)
+    g_c = {d: send(gcs.at[block(d)], gcr.at[block(d)], gc_s.at[d], gc_r.at[d], c=1 - c) for d in order}
     small[...] = jnp.zeros_like(small)
     small[0:3, :] = gro[0:3, 0:width]
     small[3:6, :] = gro[0:3, width:]
@@ -408,14 +411,18 @@
     ]
     smrecv_cx[group] = small[...]
     gown[...] = dot(jt[rows(384 * c, 384), :], dpre)
-    g_c.wait()
-    gown[...] += gcr[...].astype(F32)
-    gxs[...] = gown[...].astype(BF)
     qw = 2 * width // NX
-    gx = [
-        send(gxs.at[:, lanes(lax.rem(quarter + d, NX) * qw, qw)], gxr.at[d], gr_s.at[3, d], gr_r.at[3, d], **along(d))
-        for d in range(1, NX)
-    ]
+    gx = {}
+    for d in order:
+        g_c[d].wait()
+        gsum = gown[block(d), :] + gcr[block(d), :].astype(F32)
+        gown[block(d), :] = gsum
+        gxs[block(d), :] = gsum.astype(BF)
+        gx[d] = [
+            send(gxs.at[block(d), lanes(lax.rem(quarter + k, NX) * qw, qw)], gxr.at[k, block(d)],
+                 gx_s.at[k, d], gx_r.at[k, d], **along(k))
+            for k in range(1, NX)
+        ]
     done(sm_cps)
     acc_s = sum_of(smrecv_cx, 8)
     smy[...] = acc_s
@@ -423,6 +430,15 @@
     sm_cps = [
         send(smy, smrecv_y.at[y], gr_s.at[4, d], gr_r.at[4, d], y=lax.rem(y + d, NY)) for d in range(1, NY)
     ]
+    gz = []
+    for d in order:
+        done(gx[d])
+        acc_g = gown[block(d), lanes(quarter * qw, qw)]
+        for k in range(1, NX):
+            acc_g += gxr[k, block(d), :].astype(F32)
+        gzs[block(d), :] = acc_g.astype(BF)
+        if d:
+            gz.append((d, send(gzs.at[block(d)], gzr.at[d], gr_s.at[6, d], gr_r.at[6, d], z=lax.rem(z + d, NZ))))
     done(sm_cps)
     acc_s = sum_of(smrecv_y, NY)
     smz[...] = acc_s
@@ -430,27 +446,17 @@
     sm_cps = [
         send(smz, smrecv_z.at[z], gr_s.at[5, d], gr_r.at[5, d], z=lax.rem(z + d, NZ)) for d in range(1, NZ)
     ]
-    acc_g = gown[:, lanes(quarter * qw, qw)]
-    for d, cp in enumerate(gx):
+    for d, cp in gz:
         cp.wait()
-        acc_g += gxr[d + 1].astype(F32)
-    gzs[...] = acc_g.astype(BF)
-    gz = [
-        send(gzs.at[rows(lax.rem(z + d, NZ) * 48, 48)], gzr.at[d], gr_s.at[6, d], gr_r.at[6, d], z=lax.rem(z + d, NZ))
-        for d in range(1, NZ)
-    ]
+        acc_g += gzr[d].astype(F32)
+    gys[0] = acc_g.astype(BF)
+    g_b = [send(gys.at[0], gyr.at[0, d], gr_s.at[7, d], gr_r.at[7, d], **across(d)) for d in range(1, NY)]
     done(sm_cps)
     acc_s = sum_of(smrecv_z, NZ)
     gro_out[:, 0:width] = acc_s[0:3]
     gro_out[:, width:] = acc_s[3:6]
     loss_out[...] = acc_s[6:7, 0:1] / (3.0 * rays_total)
-    acc_g = gzs[rows(z * 48, 48), :].astype(F32)
-    for d, cp in enumerate(gz):
-        cp.wait()
-        acc_g += gzr[d + 1].astype(F32)
-    gys[0] = acc_g.astype(BF)
-    for cp in [send(gys.at[0], gyr.at[0, d], gr_s.at[7, d], gr_r.at[7, d], **across(d)) for d in range(1, NY)]:
-        cp.wait()
+    done(g_b)
     place = x * c + y * (1 - c)
     gfs[...] = ordered(gyr, gys, 0, place, NY)
 
@@ -546,7 +552,7 @@
             V((384, 2 * width), BF), V((NX, 384, width // 2), BF), V((384, width // 2), BF), V((NZ, 48, width // 2), BF),
             V((1, 48, width // 2), BF), V((1, NY, 48, width // 2), BF), V((48, width // 2), F32), V((NX, 24, width // 2), F32),
             S((5, 7)), S((5, 7)), S((5, 8)), S((5, 8)), S((5, 4, 8)), S((5, 4, 8)), S((5, 8)), S((5, 8)),
-            S((3, 32)), S((3, 32)), S((9, 8)), S((9, 8)),
+            S((3, 32)), S((3, 32)), S((9, 8)), S((9, 8)), S((8,)), S((8,)), S((4, 8)), S((4, 8)),
         ]
     )
     out = pl.pallas_call(

time: 174 us -> 161 us (0.925)
  Pallas kernels: 168 us -> 155 us
    pallas_call x1, Pallas kernels: 168 us -> 155 us  [on_device(): pl.pallas_call(kernel, out_shape=[jax.ShapeDtypeStruct((64, width), F32),...]
where the time goes in v4:
time: 161 us
  Pallas kernels  155 us (96%)
  local copies, waits for them, and re-layouts  3.59 us (2%)
  between operations  2.44 us (2%)
    pallas_call x1, Pallas kernels, on_device(): pl.pallas_call(kernel, out_shape=[jax.ShapeDtypeStruct((64, width), F32),...  155 us
    unnamed x10, local copies, waits for them, and re-layouts  3.59 us

profile of v4, /device:TPU:1, one launch (start us, length us, event | category | flops | bytes accessed | tf_op | source)
XLA Modules:
  0.0 160.7 jit_solution(9683787921990539002)
XLA Ops:
  0.6 154.7 %shard_map.191 = (f32[64,768]{1,0:T(8,128)}, f32[3,256]{1,0:T(4,128)}, f32[1,1]{1,0:T(1,128)}, f32[12,1536]{1,0:T(8,128)}, f32[3,1536]{1,0:T(4,128)}) custom-call(s32[1,256]{1,0:T(1,128)} %bitcast.3, s32[1,256]{1,0:T(1,128)} %bitcast.4, bf16[256,768]{1,0:T(8,128)(2,1)} %patches.1, bf16[256,768]{1,0:T(8,128)(2,1)} %rays.1, f32[3,256]{1,0:T(4,128)} %targets.1, ...), custom_call_target="tpu_custom_call" | custom-call | tf_op jit(solution)/shard_map/pallas_call | solution.py:558
  155.3 0.0 copy-start.2
  155.3 0.0 copy-start
  155.4 1.6 %copy.26 = f32[64,768]{1,0:T(8,128)} copy(f32[64,768]{1,0:T(8,128)} %get-tuple-element.20) | data formatting | bytes 393216
  157.0 0.0 copy-done.2
  157.0 0.6 copy.27
  158.2 0.0 copy-done
  158.2 0.0 copy-start.1
  158.2 0.6 copy.29
  158.9 0.1 copy-done.1
  159.0 0.6 copy.30
Async XLA Ops:
  155.3 1.7 %copy-start.2 = (f32[3,256]{1,0:T(4,128)S(1)}, f32[3,256]{1,0:T(4,128)}, u32[]{:S(2)}) copy-start(f32[3,256]{1,0:T(4,128)} %get-tuple-element.21) | copy-start | bytes 9220
  155.3 2.9 %copy-start = (f32[12,1536]{1,0:T(8,128)S(1)}, f32[12,1536]{1,0:T(8,128)}, u32[]{:S(2)}) copy-start(f32[12,1536]{1,0:T(8,128)} %get-tuple-element.23) | copy-start | bytes 221188
  158.2 0.7 copy-start.1

commit v5 on v4

--- a/solution.py
+++ b/solution.py
@@ -255,8 +255,6 @@
     pack_colour(3 * width)
     cy_b3 = start_bundle(3)
     c_b0 = swap_core(0, x_b0)
-    bulk = ring_x([(1, z_b1), (2, z_b2)])
-    z_b3 = start_z(3, cy_b3, ring=False)
     done(x_cam)
     cam_half = camf.at[:, lanes(c * half, half)]
     done([send(cam_half, cam_half, c_s.at[4, 0], c_r.at[4, 0], c=1 - c)])
@@ -266,8 +264,6 @@
         return dot(onehot(v == view[...]), camf[...], 0, 0)
 
     px[...] = normalize(patches[...].astype(F32) + lookup(pview)).astype(BF)
-    rin[...] = rays[...].astype(F32) + lookup(rview)
-    rx[...] = rin[...].astype(BF)
     done(c_b0)
 
     def slot_projection(normed):
@@ -279,7 +275,7 @@
     state[...] = slots_init[mine, :]
     proj = slot_projection(n0)
     x_b3, c_b3 = [], []
-    gaps = ((0, 1, 2), (3, 4, 5), (6, 7))
+    gaps = ((0, 1, 2, 3), (4, 5, 6, 7), ())
 
     def group_rows(buf, t):
         return jnp.concatenate([buf[t, g].astype(F32) for g in range(8)], axis=0)
@@ -304,6 +300,9 @@
         for k, (dc, dx) in enumerate(cx_peers()):
             cc, xx = flip(dc), lax.rem(x + dx, NX)
             cps.append(send(tsend.at[t, cc * NX + xx], trecv.at[t, k], it_s.at[t, k], it_r.at[t, k], c=cc, x=xx))
+        if t == 0:
+            bulk = ring_x([(1, z_b1), (2, z_b2)])
+            z_b3 = start_z(3, cy_b3, ring=False)
         acc = tsend[t, group].astype(F32)
         for k, cp in enumerate(cps):
             cp.wait()
@@ -331,6 +330,18 @@
             if d:
                 z_b3[d - 1].wait()
             x_b3.append((d, forward_x(3, piece(3, lax.rem(z - d + NZ, NZ)), d)))
+        if t == 1:
+            rin[...] = rays[...].astype(F32) + lookup(rview)
+            rx[...] = rin[...].astype(BF)
+        if t == 2:
+            done(c_b3)
+            r = lax.broadcasted_iota(jnp.int32, (width, 1), 0)
+            hid = 2 * r - r % 12
+            unit = lax.broadcasted_iota(jnp.int32, (width, 2 * width), 1)
+            ro[...] = (
+                dot(f3[:, 3 * width : 3 * width + 128], onehot(unit == hid), 0, 0)
+                + dot(f3[:, 3 * width + 128 : 3 * width + 256], onehot(unit == hid + 12), 0, 0)
+            )[0:8].astype(BF)
         for cp in cps:
             cp.wait()
         acc = ordered(tzrecv, tzsend, t, z, NZ)
@@ -359,16 +370,8 @@
         send(ssend, srecv.at[mine], gr_s.at[0, k], gr_r.at[0, k], c=flip(dc), x=lax.rem(x + dx, NX))
         for k, (dc, dx) in enumerate(cx_peers())
     ]
-    done(c_b3 + swap_core(3, (x_b3, [])))
     slot_keys = dot(slots.astype(BF), f1[:, width : 2 * width]).astype(BF)
     r_cps = share(t, (dot(slot_keys, f3[:, 0:width], 1, 1) * scale).astype(BF))
-    r = lax.broadcasted_iota(jnp.int32, (width, 1), 0)
-    hid = 2 * r - r % 12
-    unit = lax.broadcasted_iota(jnp.int32, (width, 2 * width), 1)
-    ro[...] = (
-        dot(f3[:, 3 * width : 3 * width + 128], onehot(unit == hid), 0, 0)
-        + dot(f3[:, 3 * width + 128 : 3 * width + 256], onehot(unit == hid + 12), 0, 0)
-    )[0:8].astype(BF)
     done(s_cps)
     done(r_cps)
     slots_all = srecv[...]

time: 161 us -> 160 us (level)
  no operation moved by 1% of the time
where the time goes in v5:
time: 160 us
  Pallas kernels  154 us (96%)
  local copies, waits for them, and re-layouts  3.59 us (2%)
  between operations  2.44 us (2%)
    pallas_call x1, Pallas kernels, on_device(): pl.pallas_call(kernel, out_shape=[jax.ShapeDtypeStruct((64, width), F32),...  154 us
    unnamed x10, local copies, waits for them, and re-layouts  3.59 us

profile of v5, /device:TPU:1, one launch (start us, length us, event | category | flops | bytes accessed | tf_op | source)
XLA Modules:
  0.0 159.8 jit_solution(1964109049900383470)
XLA Ops:
  0.6 153.8 %shard_map.191 = (f32[64,768]{1,0:T(8,128)}, f32[3,256]{1,0:T(4,128)}, f32[1,1]{1,0:T(1,128)}, f32[12,1536]{1,0:T(8,128)}, f32[3,1536]{1,0:T(4,128)}) custom-call(s32[1,256]{1,0:T(1,128)} %bitcast.3, s32[1,256]{1,0:T(1,128)} %bitcast.4, bf16[256,768]{1,0:T(8,128)(2,1)} %patches.1, bf16[256,768]{1,0:T(8,128)(2,1)} %rays.1, f32[3,256]{1,0:T(4,128)} %targets.1, ...), custom_call_target="tpu_custom_call" | custom-call | tf_op jit(solution)/shard_map/pallas_call | solution.py:561
  154.4 0.0 copy-start.2
  154.5 0.0 copy-start
  154.5 1.6 %copy.26 = f32[64,768]{1,0:T(8,128)} copy(f32[64,768]{1,0:T(8,128)} %get-tuple-element.20) | data formatting | bytes 393216
  156.1 0.0 copy-done.2
  156.1 0.6 copy.27
  157.3 0.0 copy-done
  157.4 0.0 copy-start.1
  157.4 0.6 copy.29
  158.0 0.1 copy-done.1
  158.1 0.6 copy.30
Async XLA Ops:
  154.4 1.7 %copy-start.2 = (f32[3,256]{1,0:T(4,128)S(1)}, f32[3,256]{1,0:T(4,128)}, u32[]{:S(2)}) copy-start(f32[3,256]{1,0:T(4,128)} %get-tuple-element.21) | copy-start | bytes 9220
  154.5 2.9 %copy-start = (f32[12,1536]{1,0:T(8,128)S(1)}, f32[12,1536]{1,0:T(8,128)}, u32[]{:S(2)}) copy-start(f32[12,1536]{1,0:T(8,128)} %get-tuple-element.23) | copy-start | bytes 221188
  157.4 0.7 copy-start.1

commit v6 on v5

--- a/solution.py
+++ b/solution.py
@@ -184,9 +184,13 @@
     def forward_x(b, ref, d):
         return [send(ref, ref, x_s.at[b, k, d], x_r.at[b, k, d], **along(k)) for k in range(1, NX)]
 
-    def ring_x(bundles):
-        out = {b: [(0, forward_x(b, piece(b, z), 0))] for b, _ in bundles}
-        sent = {b: list(first) for b, first in bundles}
+    out, sent = {}, {}
+
+    def ring_steps(bundles):
+        for b, first in bundles:
+            out[b] = [(0, forward_x(b, piece(b, z), 0))]
+            sent[b] = list(first)
+        yield
         for k in range(1, NZ // 2 + 1):
             for d in (k, NZ - k) if k < NZ // 2 else (k,):
                 for b, _ in bundles:
@@ -200,7 +204,7 @@
                     if d > NZ // 2 + 1:
                         sent[b].append(pass_on(b, zz, d - 1))
                     out[b].append((d, forward_x(b, piece(b, zz), d)))
-        return {b: (out[b], sent[b]) for b, _ in bundles}
+            yield
 
     def swap_core(b, gathered):
         arriving, sent = gathered
@@ -244,26 +248,31 @@
     cy_b1 = start_bundle(1)
     pack(2, (gi, gh))
     cy_b2 = start_bundle(2)
-    x_b0 = ring_x([(0, z_b0)])[0]
+    for _ in ring_steps([(0, z_b0)]):
+        pass
     z_b1 = start_z(1, cy_b1)
     z_b2 = start_z(2, cy_b2)
     x_cam = forward_x(4, cam_piece(z), 0)
     for d in range(1, NZ):
         z_cam[d - 1].wait()
         x_cam += forward_x(4, cam_piece(lax.rem(z - d + NZ, NZ)), d)
+    ring = ring_steps([(1, z_b1), (2, z_b2)])
+    next(ring)
+    c_b0 = swap_core(0, (out[0], sent[0]))
+    next(ring)
+    done(x_cam)
+    cam_half = camf.at[:, lanes(c * half, half)]
+    done([send(cam_half, cam_half, c_s.at[4, 0], c_r.at[4, 0], c=1 - c)])
+
+    def lookup(view):
+        v = lax.broadcasted_iota(jnp.int32, (camf.shape[0], view.shape[1]), 0)
+        return dot(onehot(v == view[...]), camf[...], 0, 0)
+
+    px[...] = normalize(patches[...].astype(F32) + lookup(pview)).astype(BF)
+    next(ring)
     pack(3, (mq, rin_w))
     pack_colour(3 * width)
     cy_b3 = start_bundle(3)
-    c_b0 = swap_core(0, x_b0)
-    done(x_cam)
-    cam_half = camf.at[:, lanes(c * half, half)]
-    done([send(cam_half, cam_half, c_s.at[4, 0], c_r.at[4, 0], c=1 - c)])
-
-    def lookup(view):
-        v = lax.broadcasted_iota(jnp.int32, (camf.shape[0], view.shape[1]), 0)
-        return dot(onehot(v == view[...]), camf[...], 0, 0)
-
-    px[...] = normalize(patches[...].astype(F32) + lookup(pview)).astype(BF)
     done(c_b0)
 
     def slot_projection(normed):
@@ -301,7 +310,8 @@
             cc, xx = flip(dc), lax.rem(x + dx, NX)
             cps.append(send(tsend.at[t, cc * NX + xx], trecv.at[t, k], it_s.at[t, k], it_r.at[t, k], c=cc, x=xx))
         if t == 0:
-            bulk = ring_x([(1, z_b1), (2, z_b2)])
+            for _ in ring:
+                pass
             z_b3 = start_z(3, cy_b3, ring=False)
         acc = tsend[t, group].astype(F32)
         for k, cp in enumerate(cps):
@@ -321,8 +331,8 @@
             for d in range(1, NZ)
         ]
         if t == 0:
-            c_b1 = swap_core(1, bulk[1])
-            c_b2 = swap_core(2, bulk[2])
+            c_b1 = swap_core(1, (out[1], sent[1]))
+            c_b2 = swap_core(2, (out[2], sent[2]))
         if t:
             c_b3 += swap_core(3, (x_b3, []))
             x_b3 = []

time: 160 us -> 152 us (0.950)
  Pallas kernels: 154 us -> 146 us
    pallas_call x1, Pallas kernels: 154 us -> 146 us  [on_device(): pl.pallas_call(kernel, out_shape=[jax.ShapeDtypeStruct((64, width), F32),...]
where the time goes in v6:
time: 152 us
  Pallas kernels  146 us (96%)
  local copies, waits for them, and re-layouts  3.59 us (2%)
  between operations  2.44 us (2%)
    pallas_call x1, Pallas kernels, on_device(): pl.pallas_call(kernel, out_shape=[jax.ShapeDtypeStruct((64, width), F32),...  146 us
    unnamed x10, local copies, waits for them, and re-layouts  3.59 us

profile of v6, /device:TPU:1, one launch (start us, length us, event | category | flops | bytes accessed | tf_op | source)
XLA Modules:
  0.0 152.2 jit_solution(14629963417750316621)
XLA Ops:
  0.6 146.2 %shard_map.191 = (f32[64,768]{1,0:T(8,128)}, f32[3,256]{1,0:T(4,128)}, f32[1,1]{1,0:T(1,128)}, f32[12,1536]{1,0:T(8,128)}, f32[3,1536]{1,0:T(4,128)}) custom-call(s32[1,256]{1,0:T(1,128)} %bitcast.3, s32[1,256]{1,0:T(1,128)} %bitcast.4, bf16[256,768]{1,0:T(8,128)(2,1)} %patches.1, bf16[256,768]{1,0:T(8,128)(2,1)} %rays.1, f32[3,256]{1,0:T(4,128)} %targets.1, ...), custom_call_target="tpu_custom_call" | custom-call | tf_op jit(solution)/shard_map/pallas_call | solution.py:571
  146.8 0.0 copy-start.2
  146.8 0.0 copy-start
  146.9 1.6 %copy.26 = f32[64,768]{1,0:T(8,128)} copy(f32[64,768]{1,0:T(8,128)} %get-tuple-element.20) | data formatting | bytes 393216
  148.5 0.0 copy-done.2
  148.5 0.6 copy.27
  149.7 0.0 copy-done
  149.7 0.0 copy-start.1
  149.7 0.6 copy.29
  150.4 0.1 copy-done.1
  150.5 0.6 copy.30
Async XLA Ops:
  146.8 1.7 %copy-start.2 = (f32[3,256]{1,0:T(4,128)S(1)}, f32[3,256]{1,0:T(4,128)}, u32[]{:S(2)}) copy-start(f32[3,256]{1,0:T(4,128)} %get-tuple-element.21) | copy-start | bytes 9220
  146.8 2.9 %copy-start = (f32[12,1536]{1,0:T(8,128)S(1)}, f32[12,1536]{1,0:T(8,128)}, u32[]{:S(2)}) copy-start(f32[12,1536]{1,0:T(8,128)} %get-tuple-element.23) | copy-start | bytes 221188
  149.7 0.7 copy-start.1

commit v7 on v6

--- a/solution.py
+++ b/solution.py
@@ -94,7 +94,6 @@
     for dz in range(1, NZ):
         pl.semaphore_signal(barrier, inc=1, device_id={"z": lax.rem(z + dz, NZ)}, device_id_type=pl.DeviceIdType.MESH)
         met += 1
-    pl.semaphore_wait(barrier, met)
 
     me_yc = y * 2 + c
     quarter = x * (1 - c) + y * c
@@ -224,9 +223,14 @@
 
     half = width // 2
     pack(0, (wq, wk))
-    cy_b0 = start_bundle(0)
+    pack(1, (wv, mk))
+    pack(2, (gi, gh))
+    pack(3, (mq, rin_w))
+    pack_colour(3 * width)
     camsg[...] = jnp.zeros_like(camsg)
     camsg[0:8, :] = camera[...]
+    pl.semaphore_wait(barrier, met)
+    cy_b0 = start_bundle(0)
     camcy[rows(me_yc * 16, 16), :] = camsg[:, lanes(c * half, half)]
     cy_cam = yc_copies(camsg, camcy, 4, half, lambda yy, cc: cc)
     for cp, _, _ in cy_cam:
@@ -244,9 +248,7 @@
         send(cam_piece(z), cam_piece(z), z_s.at[4, d], z_r.at[4, d], z=lax.rem(z + d, NZ))
         for d in range(1, NZ)
     ]
-    pack(1, (wv, mk))
     cy_b1 = start_bundle(1)
-    pack(2, (gi, gh))
     cy_b2 = start_bundle(2)
     for _ in ring_steps([(0, z_b0)]):
         pass
@@ -270,8 +272,6 @@
 
     px[...] = normalize(patches[...].astype(F32) + lookup(pview)).astype(BF)
     next(ring)
-    pack(3, (mq, rin_w))
-    pack_colour(3 * width)
     cy_b3 = start_bundle(3)
     done(c_b0)
 

time: 152 us -> 153 us (level)
  no operation moved by 1% of the time
where the time goes in v7:
time: 153 us; the launch traced here: 152 us
  Pallas kernels  146 us (95%)
  local copies, waits for them, and re-layouts  3.59 us (2%)
  between operations  2.44 us (2%)
    pallas_call x1, Pallas kernels, on_device(): pl.pallas_call(kernel, out_shape=[jax.ShapeDtypeStruct((64, width), F32),...  146 us
    unnamed x10, local copies, waits for them, and re-layouts  3.59 us

profile of v7, /device:TPU:1, one launch (start us, length us, event | category | flops | bytes accessed | tf_op | source)
XLA Modules:
  0.0 152.3 jit_solution(5439860011929155953)
XLA Ops:
  0.6 146.3 %shard_map.191 = (f32[64,768]{1,0:T(8,128)}, f32[3,256]{1,0:T(4,128)}, f32[1,1]{1,0:T(1,128)}, f32[12,1536]{1,0:T(8,128)}, f32[3,1536]{1,0:T(4,128)}) custom-call(s32[1,256]{1,0:T(1,128)} %bitcast.3, s32[1,256]{1,0:T(1,128)} %bitcast.4, bf16[256,768]{1,0:T(8,128)(2,1)} %patches.1, bf16[256,768]{1,0:T(8,128)(2,1)} %rays.1, f32[3,256]{1,0:T(4,128)} %targets.1, ...), custom_call_target="tpu_custom_call" | custom-call | tf_op jit(solution)/shard_map/pallas_call | solution.py:571
  147.0 0.0 copy-start.2
  147.0 0.0 copy-start
  147.0 1.6 %copy.26 = f32[64,768]{1,0:T(8,128)} copy(f32[64,768]{1,0:T(8,128)} %get-tuple-element.20) | data formatting | bytes 393216
  148.6 0.0 copy-done.2
  148.6 0.6 copy.27
  149.9 0.0 copy-done
  149.9 0.0 copy-start.1
  149.9 0.6 copy.29
  150.5 0.1 copy-done.1
  150.6 0.6 copy.30
Async XLA Ops:
  147.0 1.7 %copy-start.2 = (f32[3,256]{1,0:T(4,128)S(1)}, f32[3,256]{1,0:T(4,128)}, u32[]{:S(2)}) copy-start(f32[3,256]{1,0:T(4,128)} %get-tuple-element.21) | copy-start | bytes 9220
  147.0 2.9 %copy-start = (f32[12,1536]{1,0:T(8,128)S(1)}, f32[12,1536]{1,0:T(8,128)}, u32[]{:S(2)}) copy-start(f32[12,1536]{1,0:T(8,128)} %get-tuple-element.23) | copy-start | bytes 221188
  149.9 0.7 copy-start.1
